TPU v7x, 32 devices: a whole 2x2x4 slice. The times are simulated.
32 devices in a mesh: grp: 2 (over core), seq: 16 (over z, y, x).
Axes of the slice: x: 2, y: 2, z: 4, core: 2. Of those that a mesh axis runs over, the one named last changes fastest.
Arguments:
- prompt_x: bfloat16 [2, 2, 2048, 1024], P(None, 'grp', 'seq'), may hold values from -6 to 6
- cont_x: bfloat16 [2, 2, 64, 512, 1024], P(None, 'grp', 'seq'), may hold values from -6 to 6
- prompt_routes: int32 [2, 2, 2, 128], P(None, 'grp'), may hold values from 0 to 1023, as said below
- cont_routes: int32 [2, 2, 64, 64], P(None, 'grp', 'seq'), may hold values from 0 to 511, as said below
- cont_group: int32 [2, 2, 64], P(None, 'grp', 'seq'), may hold values from 0 to 1, as said below
- w_query: bfloat16 [1024, 1024], P(('grp', 'seq')), may hold values from -0.1875 to 0.1875
- w_key: bfloat16 [1024, 1024], P(('grp', 'seq')), may hold values from -0.1875 to 0.1875
- w_value: bfloat16 [1024, 1024], P(('grp', 'seq')), may hold values from -0.1875 to 0.1875
- w_out: bfloat16 [1024, 1024], P(('grp', 'seq')), may hold values from -1.5 to 1.5
- w_up: bfloat16 [1024, 4096], P(('grp', 'seq')), may hold values from -0.1875 to 0.1875
- w_down: bfloat16 [4096, 1024], P(('grp', 'seq')), may hold values from -0.09375 to 0.09375
- gain_attn: bfloat16 [1024], P(('grp', 'seq')), may hold values from 0.5 to 1.5
- gain_mlp: bfloat16 [1024], P(('grp', 'seq')), may hold values from 0.5 to 1.5
- w_router: bfloat16 [1024], P(('grp', 'seq')), may hold values from -0.1875 to 0.1875
- prompt_cot: bfloat16 [2, 2, 2048, 1024], P(None, 'grp', 'seq'), may hold values from -6 to 6
- cont_cot: bfloat16 [2, 2, 64, 512, 1024], P(None, 'grp', 'seq'), may hold values from -6 to 6
Outputs:
- prompt_out: bfloat16 [2, 2, 2048, 1024], P(None, 'grp', 'seq')
- cont_out: bfloat16 [2, 2, 64, 512, 1024], P(None, 'grp', 'seq')
- prompt_grad: bfloat16 [2, 2, 2048, 1024], P(None, 'grp', 'seq')
- cont_grad: bfloat16 [2, 2, 64, 512, 1024], P(None, 'grp', 'seq')
- grad_query: float32 [1024, 1024], P(('grp', 'seq'))
- grad_key: float32 [1024, 1024], P(('grp', 'seq'))
- grad_value: float32 [1024, 1024], P(('grp', 'seq'))
- grad_out: float32 [1024, 1024], P(('grp', 'seq'))
- grad_up: float32 [1024, 4096], P(('grp', 'seq'))
- grad_down: float32 [4096, 1024], P(('grp', 'seq'))
- grad_gain_attn: float32 [1024], P(('grp', 'seq'))
- grad_gain_mlp: float32 [1024], P(('grp', 'seq'))
- grad_router: float32 [1024], P(('grp', 'seq'))
Inputs may be any that keep to these rules, and one draw needn't show every extreme that they name: `prompt_routes`: each row lists 128 distinct positions of one prompt in increasing order, always including the first and the last; the 128 positions k * 128 to (k + 1) * 128 - 1 hold at most 24 of them for every k, and exactly 24 for some k in every row. `cont_routes`: each row lists 64 distinct positions of one continuation in increasing order, always including the first and the last. `cont_group`: in each micro-batch and grp index, half of the 64 continuations name prompt 0 and half name prompt 1.
All inputs are finite; a program needn't handle non-finite values.
Results may differ from a plain program's by a relative error of at most 0.017.
Values may be sent and summed in bfloat16 or wider, within the bound.
A program may use at most 320 MiB of HBM per device.

v0:
```python
import jax
import jax.numpy as jnp
from jax import lax
from jax.sharding import PartitionSpec as P

HD = 64


EPS = 1e-05
SCALE = 0.125
NEGATIVE = -1e30
ROOT = 0.7978845608028654


def normed(values, gain_vec):
    return values * lax.rsqrt(jnp.mean(values * values, -1, keepdims=True) + EPS) * gain_vec


def gelu_tanh(values):
    return 0.5 * values * (1.0 + jnp.tanh(ROOT * (values + 0.044715 * values * values * values)))


def slot_table(routes, seq_count, p_dev, pcap):
    prompt_len = p_dev * seq_count // 2
    routed_len = routes.shape[1]
    owners = jnp.arange(seq_count, dtype=jnp.int32)
    owner_prompt = owners // (seq_count // 2)
    owner_base = owners * p_dev - owner_prompt * prompt_len
    owner_routes = routes[owner_prompt]
    below = jnp.sum((owner_routes < owner_base[:, None]).astype(jnp.int32), 1)
    inside = jnp.sum((owner_routes < (owner_base + p_dev)[:, None]).astype(jnp.int32), 1) - below
    slot_ids = jnp.arange(pcap, dtype=jnp.int32)
    slot_rank = below[:, None] + slot_ids[None, :]
    slot_valid = slot_ids[None, :] < inside[:, None]
    picked = jnp.take_along_axis(owner_routes, jnp.clip(slot_rank, 0, routed_len - 1), 1)
    places = jnp.clip(picked - owner_base[:, None], 0, p_dev - 1)
    slot_group = jnp.broadcast_to(owner_prompt[:, None], slot_rank.shape)
    return (slot_group, slot_rank, slot_valid, places)


def pairwise(first_set, second_set):
    return tuple((left_arr + right_arr for left_arr, right_arr in zip(first_set, second_set)))


def body(
    prompt_x,
    cont_x,
    prompt_routes,
    cont_routes,
    cont_group,
    w_query,
    w_key,
    w_value,
    w_out,
    w_up,
    w_down,
    gain_attn,
    gain_mlp,
    w_router,
    prompt_cot,
    cont_cot,
):
    seq_count = lax.axis_size("seq")
    seq_index = lax.axis_index("seq")
    micro = prompt_x.shape[0]
    p_dev = prompt_x.shape[2]
    width = prompt_x.shape[3]
    conts = cont_x.shape[2]
    routed = cont_routes.shape[3]
    pcap = 3 * p_dev // 16
    heads = width // HD
    prompt_slots = seq_count * pcap
    shards = (w_query, w_key, w_value, w_out, w_up, w_down, gain_attn, gain_mlp, w_router)
    cont_ids = jnp.repeat(jnp.arange(conts, dtype=jnp.int32), routed)
    cont_ranks = jnp.tile(jnp.arange(routed, dtype=jnp.int32), conts)
    cont_rows_idx = jnp.arange(conts, dtype=jnp.int32)[:, None]
    totals = None
    prompt_outs = []
    cont_outs = []
    prompt_grads = []
    cont_grads = []
    for micro_step in range(micro):
        gathered = (
            lax.all_gather(shards[0], ("grp", "seq"), axis=0, tiled=True),
            lax.all_gather(shards[1], ("grp", "seq"), axis=0, tiled=True),
            lax.all_gather(shards[2], ("grp", "seq"), axis=0, tiled=True),
            lax.all_gather(shards[3], ("grp", "seq"), axis=0, tiled=True),
            lax.all_gather(shards[4], ("grp", "seq"), axis=0, tiled=True),
            lax.all_gather(shards[5], ("grp", "seq"), axis=0, tiled=True),
            lax.all_gather(shards[6], ("grp", "seq"), axis=0, tiled=True),
            lax.all_gather(shards[7], ("grp", "seq"), axis=0, tiled=True),
            lax.all_gather(shards[8], ("grp", "seq"), axis=0, tiled=True),
        )
        (
            query_mat,
            key_mat,
            value_mat,
            out_mat,
            up_mat,
            down_mat,
            attn_gain,
            mlp_gain,
            router_vec,
        ) = gathered
        attn_gain32 = attn_gain.astype(jnp.float32)
        mlp_gain32 = mlp_gain.astype(jnp.float32)
        router32 = router_vec.astype(jnp.float32)
        routes = prompt_routes[micro_step, 0]
        slot_group, slot_rank, slot_valid, places = slot_table(routes, seq_count, p_dev, pcap)
        own_group = lax.dynamic_index_in_dim(slot_group, seq_index, 0, keepdims=False)
        own_rank = lax.dynamic_index_in_dim(slot_rank, seq_index, 0, keepdims=False)
        own_valid = lax.dynamic_index_in_dim(slot_valid, seq_index, 0, keepdims=False)
        own_places = lax.dynamic_index_in_dim(places, seq_index, 0, keepdims=False)
        drop_places = jnp.where(own_valid, own_places, p_dev)
        cont_index = cont_routes[micro_step, 0]
        cont_prompt = cont_group[micro_step, 0]
        prompt_local = prompt_x[micro_step, 0]
        cont_local = cont_x[micro_step, 0]
        token_rows = jnp.concatenate(
            [
                jnp.take(prompt_local, own_places, axis=0),
                jnp.take_along_axis(cont_local, cont_index[:, :, None], 1).reshape(
                    conts * routed, width
                ),
            ],
            0,
        )
        query_group = jnp.concatenate([own_group, jnp.repeat(cont_prompt, routed)])
        query_cont = jnp.concatenate([jnp.full((pcap,), -1, jnp.int32), cont_ids])
        query_rank = jnp.concatenate([own_rank, cont_ranks])
        prompt_mask = (
            slot_valid.reshape(-1)[None, :]
            & (slot_group.reshape(-1)[None, :] == query_group[:, None])
            & ((query_cont[:, None] >= 0) | (slot_rank.reshape(-1)[None, :] <= query_rank[:, None]))
        )
        own_mask = (cont_ids[None, :] == query_cont[:, None]) & (
            cont_ranks[None, :] <= query_rank[:, None]
        )
        key_mask = jnp.concatenate([prompt_mask, own_mask], 1)
        rows_f = token_rows.astype(jnp.float32)
        first_b = normed(rows_f, attn_gain32).astype(jnp.bfloat16)
        query_b = jnp.dot(first_b, query_mat, preferred_element_type=jnp.float32).astype(
            jnp.bfloat16
        )
        key_b = jnp.dot(first_b, key_mat, preferred_element_type=jnp.float32).astype(jnp.bfloat16)
        value_b = jnp.dot(first_b, value_mat, preferred_element_type=jnp.float32).astype(
            jnp.bfloat16
        )
        kv_own = jnp.concatenate([key_b[:pcap], value_b[:pcap]], 1)
        kv_all = lax.all_gather(kv_own, "seq", axis=0, tiled=True)
        key_heads = jnp.concatenate([kv_all[:, :width], key_b[pcap:]], 0).reshape(-1, heads, HD)
        value_heads = jnp.concatenate([kv_all[:, width:], value_b[pcap:]], 0).reshape(-1, heads, HD)
        query_heads = query_b.reshape(-1, heads, HD)
        raw_scores = (
            jnp.einsum("qhd,khd->hqk", query_heads, key_heads, preferred_element_type=jnp.float32)
            * SCALE
        )
        masked = jnp.where(key_mask[None], raw_scores, NEGATIVE)
        row_max = jnp.max(masked, -1, keepdims=True)
        exp_scores = jnp.exp(masked - row_max)
        row_total = jnp.sum(exp_scores, -1, keepdims=True)
        attn_probs = exp_scores / row_total
        attended = jnp.einsum(
            "hqk,khd->qhd",
            attn_probs.astype(jnp.bfloat16),
            value_heads,
            preferred_element_type=jnp.float32,
        )
        attended_b = attended.reshape(-1, width).astype(jnp.bfloat16)
        branch_a = jnp.dot(attended_b, out_mat, preferred_element_type=jnp.float32)
        hidden = rows_f + branch_a
        second_b = normed(hidden, mlp_gain32).astype(jnp.bfloat16)
        up_proj = jnp.dot(second_b, up_mat, preferred_element_type=jnp.float32)
        gelu_b = gelu_tanh(up_proj).astype(jnp.bfloat16)
        branch_m = jnp.dot(gelu_b, down_mat, preferred_element_type=jnp.float32)
        router_logit = jnp.dot(token_rows, router_vec, preferred_element_type=jnp.float32)
        router_score = 1.0 / (1.0 + jnp.exp(-router_logit))
        branch_sum = branch_a + branch_m
        result = rows_f + router_score[:, None] * branch_sum
        out_b = result.astype(jnp.bfloat16)
        prompt_outs.append(prompt_local.at[drop_places].set(out_b[:pcap], mode="drop"))
        cont_outs.append(
            cont_local.at[cont_rows_idx, cont_index].set(out_b[pcap:].reshape(conts, routed, width))
        )
        gathered = (
            lax.all_gather(shards[0], ("grp", "seq"), axis=0, tiled=True),
            lax.all_gather(shards[1], ("grp", "seq"), axis=0, tiled=True),
            lax.all_gather(shards[2], ("grp", "seq"), axis=0, tiled=True),
            lax.all_gather(shards[3], ("grp", "seq"), axis=0, tiled=True),
            lax.all_gather(shards[4], ("grp", "seq"), axis=0, tiled=True),
            lax.all_gather(shards[5], ("grp", "seq"), axis=0, tiled=True),
            lax.all_gather(shards[6], ("grp", "seq"), axis=0, tiled=True),
            lax.all_gather(shards[7], ("grp", "seq"), axis=0, tiled=True),
            lax.all_gather(shards[8], ("grp", "seq"), axis=0, tiled=True),
        )
        (
            query_mat,
            key_mat,
            value_mat,
            out_mat,
            up_mat,
            down_mat,
            attn_gain,
            mlp_gain,
            router_vec,
        ) = gathered
        row_weight = jnp.concatenate([own_valid, jnp.ones((conts * routed,), dtype=bool)]).astype(
            jnp.float32
        )
        cot_rows = jnp.concatenate(
            [
                jnp.take(prompt_cot[micro_step, 0], own_places, axis=0),
                jnp.take_along_axis(cont_cot[micro_step, 0], cont_index[:, :, None], 1).reshape(
                    conts * routed, width
                ),
            ],
            0,
        )
        cot_rows = cot_rows.astype(jnp.float32) * row_weight[:, None]
        grad_score = jnp.sum(cot_rows * branch_sum, -1)
        grad_logit = grad_score * router_score * (1.0 - router_score)
        router_grad = jnp.dot(grad_logit, rows_f, precision=lax.Precision.HIGHEST)
        grad_rows = cot_rows + grad_logit[:, None] * router32[None, :]
        grad_branch = cot_rows * router_score[:, None]
        grad_m = grad_branch.astype(jnp.bfloat16)
        down_grad = jnp.einsum("qf,qd->fd", gelu_b, grad_m, preferred_element_type=jnp.float32)
        grad_gelu = jnp.einsum("qd,fd->qf", grad_m, down_mat, preferred_element_type=jnp.float32)
        gelu_back = jax.vjp(gelu_tanh, up_proj)[1]
        grad_upper = gelu_back(grad_gelu)[0].astype(jnp.bfloat16)
        up_grad = jnp.einsum("qd,qf->df", second_b, grad_upper, preferred_element_type=jnp.float32)
        grad_second = jnp.einsum(
            "qf,df->qd", grad_upper, up_mat, preferred_element_type=jnp.float32
        )
        norm_back = jax.vjp(normed, hidden, mlp_gain32)[1]
        grad_hidden, mlp_gain_grad = norm_back(grad_second)
        grad_rows = grad_rows + grad_hidden
        grad_a = (grad_branch + grad_hidden).astype(jnp.bfloat16)
        out_grad = jnp.einsum("qa,qd->ad", attended_b, grad_a, preferred_element_type=jnp.float32)
        grad_att = (
            jnp.einsum("qd,ad->qa", grad_a, out_mat, preferred_element_type=jnp.float32)
            .astype(jnp.bfloat16)
            .reshape(-1, heads, HD)
        )
        raw_scores = (
            jnp.einsum("qhd,khd->hqk", query_heads, key_heads, preferred_element_type=jnp.float32)
            * SCALE
        )
        masked = jnp.where(key_mask[None], raw_scores, NEGATIVE)
        attn_probs = jnp.exp(masked - row_max) / row_total
        probs_b = attn_probs.astype(jnp.bfloat16)
        grad_vheads = jnp.einsum(
            "hqk,qhd->khd", probs_b, grad_att, preferred_element_type=jnp.float32
        )
        grad_probs = jnp.einsum(
            "qhd,khd->hqk", grad_att, value_heads, preferred_element_type=jnp.float32
        )
        inner_sum = jnp.sum(attn_probs * grad_probs, -1, keepdims=True)
        grad_scores = (attn_probs * (grad_probs - inner_sum)).astype(jnp.bfloat16)
        grad_qheads = (
            jnp.einsum("hqk,khd->qhd", grad_scores, key_heads, preferred_element_type=jnp.float32)
            * SCALE
        )
        grad_kheads = (
            jnp.einsum("hqk,qhd->khd", grad_scores, query_heads, preferred_element_type=jnp.float32)
            * SCALE
        )
        kv_term = jnp.concatenate(
            [
                grad_kheads[:prompt_slots].reshape(prompt_slots, width),
                grad_vheads[:prompt_slots].reshape(prompt_slots, width),
            ],
            1,
        )
        kv_own_grad = lax.psum_scatter(
            kv_term.astype(jnp.bfloat16), "seq", scatter_dimension=0, tiled=True
        ).astype(jnp.float32)
        grad_key = jnp.concatenate(
            [kv_own_grad[:, :width], grad_kheads[prompt_slots:].reshape(-1, width)], 0
        ).astype(jnp.bfloat16)
        grad_value = jnp.concatenate(
            [kv_own_grad[:, width:], grad_vheads[prompt_slots:].reshape(-1, width)], 0
        ).astype(jnp.bfloat16)
        grad_query = grad_qheads.reshape(-1, width).astype(jnp.bfloat16)
        query_grad = jnp.einsum(
            "qa,qd->ad", first_b, grad_query, preferred_element_type=jnp.float32
        )
        key_grad = jnp.einsum("qa,qd->ad", first_b, grad_key, preferred_element_type=jnp.float32)
        value_grad = jnp.einsum(
            "qa,qd->ad", first_b, grad_value, preferred_element_type=jnp.float32
        )
        grad_first = (
            jnp.einsum("qd,ad->qa", grad_query, query_mat, preferred_element_type=jnp.float32)
            + jnp.einsum("qd,ad->qa", grad_key, key_mat, preferred_element_type=jnp.float32)
            + jnp.einsum("qd,ad->qa", grad_value, value_mat, preferred_element_type=jnp.float32)
        )
        first_back = jax.vjp(normed, rows_f, attn_gain32)[1]
        grad_norm_rows, attn_gain_grad = first_back(grad_first)
        grad_rows = grad_rows + grad_norm_rows
        grad_b = grad_rows.astype(jnp.bfloat16)
        prompt_grads.append(
            prompt_cot[micro_step, 0].at[drop_places].set(grad_b[:pcap], mode="drop")
        )
        cont_grads.append(
            cont_cot[micro_step, 0]
            .at[cont_rows_idx, cont_index]
            .set(grad_b[pcap:].reshape(conts, routed, width))
        )
        step_grads = (
            query_grad,
            key_grad,
            value_grad,
            out_grad,
            up_grad,
            down_grad,
            attn_gain_grad,
            mlp_gain_grad,
            router_grad,
        )
        totals = step_grads if totals is None else pairwise(totals, step_grads)
    final_grads = (
        lax.psum_scatter(totals[0], ("grp", "seq"), scatter_dimension=0, tiled=True),
        lax.psum_scatter(totals[1], ("grp", "seq"), scatter_dimension=0, tiled=True),
        lax.psum_scatter(totals[2], ("grp", "seq"), scatter_dimension=0, tiled=True),
        lax.psum_scatter(totals[3], ("grp", "seq"), scatter_dimension=0, tiled=True),
        lax.psum_scatter(totals[4], ("grp", "seq"), scatter_dimension=0, tiled=True),
        lax.psum_scatter(totals[5], ("grp", "seq"), scatter_dimension=0, tiled=True),
        lax.psum_scatter(totals[6], ("grp", "seq"), scatter_dimension=0, tiled=True),
        lax.psum_scatter(totals[7], ("grp", "seq"), scatter_dimension=0, tiled=True),
        lax.psum_scatter(totals[8], ("grp", "seq"), scatter_dimension=0, tiled=True),
    )
    return (
        jnp.stack(prompt_outs)[:, None],
        jnp.stack(cont_outs)[:, None],
        jnp.stack(prompt_grads)[:, None],
        jnp.stack(cont_grads)[:, None],
    ) + tuple(final_grads)


def solution(mesh):
    in_specs = (
        P(None, "grp", "seq", None),
        P(None, "grp", "seq", None, None),
        P(None, "grp", None, None),
        P(None, "grp", "seq", None),
        P(None, "grp", "seq"),
        P(("grp", "seq"), None),
        P(("grp", "seq"), None),
        P(("grp", "seq"), None),
        P(("grp", "seq"), None),
        P(("grp", "seq"), None),
        P(("grp", "seq"), None),
        P(("grp", "seq")),
        P(("grp", "seq")),
        P(("grp", "seq")),
        P(None, "grp", "seq", None),
        P(None, "grp", "seq", None, None),
    )
    out_specs = (
        P(None, "grp", "seq", None),
        P(None, "grp", "seq", None, None),
        P(None, "grp", "seq", None),
        P(None, "grp", "seq", None, None),
        P(("grp", "seq"), None),
        P(("grp", "seq"), None),
        P(("grp", "seq"), None),
        P(("grp", "seq"), None),
        P(("grp", "seq"), None),
        P(("grp", "seq"), None),
        P(("grp", "seq")),
        P(("grp", "seq")),
        P(("grp", "seq")),
    )
    return jax.shard_map(body, mesh=mesh, in_specs=in_specs, out_specs=out_specs, check_vma=False)
```

profile of v0, /device:TPU:0, one launch (start us, length us, event | category | flops | bytes accessed | tf_op | source)
XLA Modules:
  0.0 2181.8 jit_solution(7145114298374675107)
XLA Ops:
  15.3 42.2 %all-reduce.12 = (bf16[1024]{0:T(1024)(128)(2,1)S(1)}, bf16[1024]{0:T(1024)(128)(2,1)}, bf16[1024]{0:T(1024)(128)(2,1)S(1)}) all-reduce(bf16[1024]{0:T(1024)(128)(2,1)S(1)} %dynamic-update-slice.1, bf16[1024]{0:T(1024)(128)(2,1)S(1)} %dynamic-update-slice.2, ...), channel_id=1, replica_groups=mesh['grp'=2,'seq'=16] {'grp','seq'}, use_global_device_ids=true, to_apply=%add.6 | all-reduce | flops 3072 | bytes 12288
  100.5 27.7 %all-gather.9.cloned.1.call-done = bf16[1024,1024]{1,0:T(8,128)(2,1)} async-done(((bf16[32,1024]{1,0:T(8,128)(2,1)}), bf16[1024,1024]{1,0:T(8,128)(2,1)}) %all-gather.9.cloned.1.call-update) | async-done | bytes 2097168 | tf_op jit(solution)/shard_map/all_gather | solution.py:85
  150.3 36.2 %all-gather.15.cloned.1.call-done = bf16[1024,1024]{1,0:T(8,128)(2,1)} async-done(((bf16[32,1024]{1,0:T(8,128)(2,1)}), bf16[1024,1024]{1,0:T(8,128)(2,1)}) %all-gather.15.cloned.1.call-update) | async-done | bytes 2097168 | tf_op jit(solution)/shard_map/all_gather | solution.py:84
  193.8 52.6 %all-gather.13.cloned.1.call-done = bf16[384,2048]{1,0:T(8,128)(2,1)} async-done(((bf16[24,2048]{1,0:T(8,128)(2,1)}), bf16[384,2048]{1,0:T(8,128)(2,1)}) %all-gather.13.cloned.1.call-update) | async-done | bytes 1572880 | tf_op jit(solution)/shard_map/all_gather | solution.py:150
  249.5 56.7 %all-gather.23.cloned.1.call-done = bf16[384,2048]{1,0:T(8,128)(2,1)} async-done(((bf16[24,2048]{1,0:T(8,128)(2,1)}), bf16[384,2048]{1,0:T(8,128)(2,1)}) %all-gather.23.cloned.1.call-update) | async-done | bytes 1572880 | tf_op jit(solution)/shard_map/all_gather | solution.py:150
  315.7 10.1 fusion.150
  333.1 31.1 %all-gather.17.cloned.1.call-done = bf16[1024,1024]{1,0:T(8,128)(2,1)} async-done(((bf16[32,1024]{1,0:T(8,128)(2,1)}), bf16[1024,1024]{1,0:T(8,128)(2,1)}) %all-gather.17.cloned.1.call-update) | async-done | bytes 2097168 | tf_op jit(solution)/shard_map/all_gather | solution.py:87
  368.4 9.7 fusion.151
  387.2 56.3 %all-gather.19.cloned.1.call-done = bf16[1024,4096]{1,0:T(8,128)(2,1)} async-done(((bf16[32,4096]{1,0:T(8,128)(2,1)}), bf16[1024,4096]{1,0:T(8,128)(2,1)}) %all-gather.19.cloned.1.call-update) | async-done | bytes 8388624 | tf_op jit(solution)/shard_map/all_gather | solution.py:88
  443.5 8.1 fusion.118
  451.5 71.0 %all-gather.21.cloned.1.call-done = bf16[4096,1024]{1,0:T(8,128)(2,1)} async-done(((bf16[128,1024]{1,0:T(8,128)(2,1)}), bf16[4096,1024]{1,0:T(8,128)(2,1)}) %all-gather.21.cloned.1.call-update) | async-done | bytes 8388624 | tf_op jit(solution)/shard_map/all_gather | solution.py:89
  522.5 9.1 fusion.13
  531.6 7.6 multiply_reduce_fusion.3
  547.9 9.2 fusion.17
  581.0 9.6 multiply_reduce_fusion.1
  598.7 8.6 multiply_convert_fusion.1
  662.9 73.7 %reduce-scatter.25.cloned.1.call-done = bf16[24,2048]{1,0:T(8,128)(2,1)} async-done(((bf16[384,2048]{1,0:T(8,128)(2,1)}), bf16[24,2048]{1,0:T(8,128)(2,1)}) %reduce-scatter.25.cloned.1.call-update) | async-done | bytes 98320
  737.6 127.2 %reduce-scatter.27.cloned.1.call-done = bf16[24,2048]{1,0:T(8,128)(2,1)} async-done(((bf16[384,2048]{1,0:T(8,128)(2,1)}), bf16[24,2048]{1,0:T(8,128)(2,1)}) %reduce-scatter.27.cloned.1.call-update) | async-done | bytes 98320
  881.4 11.3 fusion.120
  892.7 13.7 convolution_add_fusion
  913.3 12.9 convolution_add_fusion.1
  931.2 36.4 %scatter_fusion.1 = bf16[4,512,1024]{2,1,0:T(8,128)(2,1)} fusion(bf16[4,512,1024]{2,1,0:T(8,128)(2,1)} %get-tuple-element.86, s32[256]{0:T(256)S(1)} %reshape.617, bf16[256,1024]{1,0:T(8,128)(2,1)S(1)} %slice.247), kind=kCustom, calls=%fused_computation.15 | custom fusion | bytes 1574912 | tf_op jit(solution)/shard_map/scatter | solution.py:183
  968.9 36.4 %scatter_fusion = bf16[4,512,1024]{2,1,0:T(8,128)(2,1)} fusion(bf16[4,512,1024]{2,1,0:T(8,128)(2,1)} %get-tuple-element.85, s32[256]{0:T(256)S(1)} %reshape.611, bf16[256,1024]{1,0:T(8,128)(2,1)S(1)} %slice.246), kind=kCustom, calls=%fused_computation.14 | custom fusion | bytes 1574912 | tf_op jit(solution)/shard_map/scatter | solution.py:183
  1012.2 7.8 maximum_bitcast_fusion
  1037.9 36.3 %scatter_fusion.3 = bf16[4,512,1024]{2,1,0:T(8,128)(2,1)} fusion(bf16[4,512,1024]{2,1,0:T(8,128)(2,1)} %get-tuple-element.84, s32[256]{0:T(256)S(1)} %reshape.617, bf16[256,1024]{1,0:T(8,128)(2,1)S(1)} %slice-done.10), kind=kCustom, calls=%fused_computation.19 | custom fusion | bytes 1574912 | tf_op jit(solution)/shard_map/scatter | solution.py:306
  1074.2 36.3 %scatter_fusion.2 = bf16[4,512,1024]{2,1,0:T(8,128)(2,1)} fusion(bf16[4,512,1024]{2,1,0:T(8,128)(2,1)} %get-tuple-element.83, s32[256]{0:T(256)S(1)} %reshape.611, bf16[256,1024]{1,0:T(8,128)(2,1)S(1)} %slice-done.9), kind=kCustom, calls=%fused_computation.18 | custom fusion | bytes 1574912 | tf_op jit(solution)/shard_map/scatter | solution.py:306
  1110.5 40.7 %all-reduce.11 = (f32[1024]{0:T(1024)S(1)}, f32[1024]{0:T(1024)S(1)}, f32[1024]{0:T(1024)S(1)}) all-reduce(f32[1024]{0:T(1024)S(1)} %add.377, f32[1024]{0:T(1024)S(1)} %copy-done.116, f32[1024]{0:T(1024)S(1)} %copy-done.117), channel_id=10, replica_groups=mesh['grp'=2,'seq'=16] {'grp','seq'}, use_global_device_ids=true, to_apply=%region_38.42.clone | all-reduce | flops 3072 | bytes 24576
  1153.9 7.7 maximum_bitcast_fusion.1
  1161.5 145.8 %reduce-scatter.17.cloned.1.call-done = f32[32,1024]{1,0:T(8,128)} async-done(((f32[1024,1024]{1,0:T(8,128)}), f32[32,1024]{1,0:T(8,128)}) %reduce-scatter.17.cloned.1.call-update) | async-done | bytes 131088 | tf_op jit(solution)/shard_map/reduce_scatter | solution.py:323
  1307.3 146.3 %reduce-scatter.15.cloned.1.call-done = f32[32,1024]{1,0:T(8,128)} async-done(((f32[1024,1024]{1,0:T(8,128)}), f32[32,1024]{1,0:T(8,128)}) %reduce-scatter.15.cloned.1.call-update) | async-done | bytes 131088 | tf_op jit(solution)/shard_map/reduce_scatter | solution.py:322
  1453.7 358.4 %reduce-scatter.23.cloned.1.call-done = f32[128,1024]{1,0:T(8,128)} async-done(((f32[4096,1024]{1,0:T(8,128)}), f32[128,1024]{1,0:T(8,128)}) %reduce-scatter.23.cloned.1.call-update) | async-done | bytes 524304 | tf_op jit(solution)/shard_map/reduce_scatter | solution.py:326
  1812.1 362.8 %reduce-scatter.21.cloned.1.call-done = f32[32,4096]{1,0:T(8,128)} async-done(((f32[1024,4096]{1,0:T(8,128)}), f32[32,4096]{1,0:T(8,128)}) %reduce-scatter.21.cloned.1.call-update) | async-done | bytes 524304 | tf_op jit(solution)/shard_map/reduce_scatter | solution.py:325
  (604 shorter events, 265.9 us)
Async XLA Ops:
  7.2 90.8 %all-gather.11.cloned.1.call-start = ((), (), s32[]{:S(2)}) async-start(), calls=%async_computation.9 | async-start | bytes 2162688 | tf_op jit(solution)/shard_map/all_gather | solution.py:86
  7.9 120.3 %all-gather.9.cloned.1.call-start = ((), (), s32[]{:S(2)}) async-start(), calls=%async_computation.8 | async-start | bytes 2162688 | tf_op jit(solution)/shard_map/all_gather | solution.py:85
  8.7 177.8 %all-gather.15.cloned.1.call-start = ((), (), s32[]{:S(2)}) async-start(), calls=%async_computation.11 | async-start | bytes 2162688 | tf_op jit(solution)/shard_map/all_gather | solution.py:84
  9.4 237.0 %all-gather.13.cloned.1.call-start = ((), (), s32[]{:S(2)}) async-start(), calls=%async_computation.10 | async-start | bytes 1671168 | tf_op jit(solution)/shard_map/all_gather | solution.py:150
  57.4 86.5 %copy-start.128 = (bf16[1024]{0:T(1024)(128)(2,1)}, bf16[1024]{0:T(1024)(128)(2,1)S(1)}, u32[]{:S(2)}) copy-start(bf16[1024]{0:T(1024)(128)(2,1)S(1)} %get-tuple-element.74) | copy-start | bytes 6148
  57.4 132.7 %copy-start.75 = (f32[1024]{0:T(1024)}, f32[1024]{0:T(1024)S(1)}, u32[]{:S(2)}) copy-start(f32[1024]{0:T(1024)S(1)} %convert_element_type.175) | copy-start | bytes 12292
  66.8 64.7 %copy-start.27 = (bf16[128,1024]{1,0:T(8,128)(2,1)}, bf16[128,1024]{1,0:T(8,128)(2,1)S(1)}, u32[]{:S(2)}) copy-start(bf16[128,1024]{1,0:T(8,128)(2,1)S(1)} %get-tuple-element.100) | copy-start | bytes 786436
  68.2 64.0 %copy-start.25 = (bf16[128,1024]{1,0:T(8,128)(2,1)}, bf16[128,1024]{1,0:T(8,128)(2,1)S(1)}, u32[]{:S(2)}) copy-start(bf16[128,1024]{1,0:T(8,128)(2,1)S(1)} %get-tuple-element.98) | copy-start | bytes 786436
  95.5 91.0 %copy-start.40 = (bf16[24,1024]{1,0:T(8,128)(2,1)}, bf16[24,1024]{1,0:T(8,128)(2,1)S(1)}, u32[]{:S(2)}) copy-start(bf16[24,1024]{1,0:T(8,128)(2,1)S(1)} %get-tuple-element.126) | copy-start | bytes 147460
  98.0 88.5 %copy-start.90 = (f32[280]{0:T(512)}, f32[280]{0:T(512)S(1)}, u32[]{:S(2)}) copy-start(f32[280]{0:T(512)S(1)} %fusion.94) | copy-start | bytes 3364
  131.4 174.8 %all-gather.23.cloned.1.call-start = ((), (), s32[]{:S(2)}) async-start(), calls=%async_computation.15 | async-start | bytes 1671168 | tf_op jit(solution)/shard_map/all_gather | solution.py:150
  133.4 56.7 %copy-start.43 = (bf16[24,1024]{1,0:T(8,128)(2,1)}, bf16[24,1024]{1,0:T(8,128)(2,1)S(1)}, u32[]{:S(2)}) copy-start(bf16[24,1024]{1,0:T(8,128)(2,1)S(1)} %get-tuple-element.130) | copy-start | bytes 147460
  138.8 225.3 %all-gather.17.cloned.1.call-start = ((), (), s32[]{:S(2)}) async-start(), calls=%async_computation.12 | async-start | bytes 2162688 | tf_op jit(solution)/shard_map/all_gather | solution.py:87
  139.4 304.0 %all-gather.19.cloned.1.call-start = ((), (), s32[]{:S(2)}) async-start(), calls=%async_computation.13 | async-start | bytes 8650752 | tf_op jit(solution)/shard_map/all_gather | solution.py:88
  140.2 382.3 %all-gather.21.cloned.1.call-start = ((), (), s32[]{:S(2)}) async-start(), calls=%async_computation.14 | async-start | bytes 8650752 | tf_op jit(solution)/shard_map/all_gather | solution.py:89
  140.9 595.7 %reduce-scatter.25.cloned.1.call-start = ((), (), s32[]{:S(2)}) async-start(), calls=%async_computation.22 | async-start | bytes 1671168
  145.5 445.1 %copy-start.103 = (f32[280]{0:T(512)}, f32[280]{0:T(512)S(1)}, u32[]{:S(2)}) copy-start(f32[280]{0:T(512)S(1)} %pad_convert_fusion) | copy-start | bytes 3364
  367.8 222.7 %copy-start.2 = (f32[280,1024]{1,0:T(8,128)}, f32[280,1024]{1,0:T(8,128)S(1)}, u32[]{:S(2)}) copy-start(f32[280,1024]{1,0:T(8,128)S(1)} %get-tuple-element.80) | copy-start | bytes 3440644
  367.9 222.7 %copy-start.97 = (f32[280]{0:T(512)}, f32[280]{0:T(512)S(1)}, u32[]{:S(2)}) copy-start(f32[280]{0:T(512)S(1)} %fusion.97) | copy-start | bytes 3364
  387.1 176.9 %copy-start.4 = (f32[280,1024]{1,0:T(8,128)}, f32[280,1024]{1,0:T(8,128)S(1)}, u32[]{:S(2)}) copy-start(f32[280,1024]{1,0:T(8,128)S(1)} %get-tuple-element.76) | copy-start | bytes 3440644
  387.1 176.9 %copy-start.95 = (f32[280]{0:T(512)}, f32[280]{0:T(512)S(1)}, u32[]{:S(2)}) copy-start(f32[280]{0:T(512)S(1)} %fusion.95) | copy-start | bytes 3364
  443.5 79.1 %copy-start.89 = (bf16[24,1024]{1,0:T(8,128)(2,1)S(1)}, bf16[24,1024]{1,0:T(8,128)(2,1)}, u32[]{:S(2)}) copy-start(bf16[24,1024]{1,0:T(8,128)(2,1)} %get-tuple-element.125) | copy-start | bytes 147460
  443.5 79.1 %copy-start.106 = (f32[280]{0:T(512)S(1)}, f32[280]{0:T(512)}, u32[]{:S(2)}) copy-start(f32[280]{0:T(512)} %pad_convert_fusion.1) | copy-start | bytes 3364
  443.5 79.1 %copy-start.126 = (f32[280]{0:T(512)S(1)}, f32[280]{0:T(512)}, u32[]{:S(2)}) copy-start(f32[280]{0:T(512)} %add_divide_fusion.1) | copy-start | bytes 3364
  613.3 251.5 %reduce-scatter.27.cloned.1.call-start = ((), (), s32[]{:S(2)}) async-start(), calls=%async_computation.23 | async-start | bytes 1671168
  635.6 525.9 %reduce-scatter.19.cloned.1.call-start = ((), (), s32[]{:S(2)}) async-start(), calls=%async_computation.19 | async-start | bytes 4325376 | tf_op jit(solution)/shard_map/reduce_scatter | solution.py:324
  642.4 519.1 %reduce-scatter.13.cloned.1.call-start = ((), (), s32[]{:S(2)}) async-start(), calls=%async_computation.16 | async-start | bytes 4325376 | tf_op jit(solution)/shard_map/reduce_scatter | solution.py:321
  660.1 647.2 %reduce-scatter.17.cloned.1.call-start = ((), (), s32[]{:S(2)}) async-start(), calls=%async_computation.18 | async-start | bytes 4325376 | tf_op jit(solution)/shard_map/reduce_scatter | solution.py:323
  737.6 131.0 %copy-start.67 = (bf16[24,1024]{0,1:T(8,128)(2,1)}, bf16[24,1024]{0,1:T(8,128)(2,1)S(1)}, u32[]{:S(2)}) copy-start(bf16[24,1024]{0,1:T(8,128)(2,1)S(1)} %copy.78) | copy-start | bytes 147460
  872.3 581.4 %reduce-scatter.15.cloned.1.call-start = ((), (), s32[]{:S(2)}) async-start(), calls=%async_computation.17 | async-start | bytes 4325376 | tf_op jit(solution)/shard_map/reduce_scatter | solution.py:322
  880.4 931.7 %reduce-scatter.23.cloned.1.call-start = ((), (), s32[]{:S(2)}) async-start(), calls=%async_computation.21 | async-start | bytes 17301504 | tf_op jit(solution)/shard_map/reduce_scatter | solution.py:326
  906.4 1268.4 %reduce-scatter.21.cloned.1.call-start = ((), (), s32[]{:S(2)}) async-start(), calls=%async_computation.20 | async-start | bytes 17301504 | tf_op jit(solution)/shard_map/reduce_scatter | solution.py:325
  (163 other events, 1254.3 us)
Sparse Core Ops, SparseCore 0:
  10.9 59.0 all-gather.10
  72.9 55.2 all-gather.8
  131.1 55.3 all-gather.14
  189.7 56.6 all-gather.12
  249.6 56.5 all-gather.22
  309.0 55.1 all-gather.16
  367.0 76.3 all-gather.18
  446.3 76.1 all-gather.20
  613.4 123.1 reduce-scatter.24
  741.3 123.5 reduce-scatter.26
  867.7 145.6 reduce-scatter.18
  1016.1 142.1 reduce-scatter.12
  1161.1 146.1 reduce-scatter.16
  1310.0 143.5 reduce-scatter.14
  1456.4 355.6 reduce-scatter.22
  1814.8 359.9 reduce-scatter.20
where the time goes:
time: 2200 us; the launch traced here: 2180 us
  waiting for transfers between devices  1550 us (70%)
  local copies, waits for them, and re-layouts  241 us (11%)
  matrix products  238 us (11%)
  blocking collectives  82.9 us (4%)
  other arithmetic  52 us (2%)
    reduce_scatter x1, waiting for transfers between devices, body(): lax.psum_scatter(totals[4], ('grp', 'seq'), scatter_dimension=0, tiled=True)  363 us
    reduce_scatter x1, waiting for transfers between devices, body(): lax.psum_scatter(totals[5], ('grp', 'seq'), scatter_dimension=0, tiled=True)  358 us
    unnamed x18, waiting for transfers between devices  205 us
    reduce_scatter x1, waiting for transfers between devices, body(): lax.psum_scatter(totals[1], ('grp', 'seq'), scatter_dimension=0, tiled=True)  146 us
    reduce_scatter x1, waiting for transfers between devices, body(): lax.psum_scatter(totals[2], ('grp', 'seq'), scatter_dimension=0, tiled=True)  146 us
    all_gather x2, waiting for transfers between devices, body(): kv_all = lax.all_gather(kv_own, 'seq', axis=0, tiled=True)  109 us
    unnamed x2, blocking collectives  82.9 us
    scatter x2, local copies, waits for them, and re-layouts, body(): cont_local.at[cont_rows_idx, cont_index]  72.8 us
  transfers between devices with their start and end apart: 16, of which 13 were waited for; matrix products, arithmetic and copies ran while one was open for 20% of the time, Pallas kernels for 0%

commit v1 on v0

v1 whole, which is shorter than its diff:
```python
import functools

import jax
import jax.numpy as jnp
from jax import lax
from jax.experimental import pallas as pl
from jax.experimental.pallas import tpu as pltpu
from jax.sharding import PartitionSpec as P

HD = 64
EPS = 1e-05
SCALE = 0.125
NEGATIVE = -1e30
ROOT = 0.7978845608028654
FAR = 1 << 20
PPAD = 32
MESH = pl.DeviceIdType.MESH
ANY = pl.BlockSpec(memory_space=pl.ANY)
BF = jnp.bfloat16
F32 = jnp.float32
ZYX = (4, 2, 2)


def coords():
    g = lax.axis_index("grp")
    s = lax.axis_index("seq")
    return g, s, s // 4, (s // 2) % 2, s % 2


def partners():
    g, s, z, y, x = coords()
    out = {
        "x": (g, z * 4 + y * 2 + (1 - x)),
        "y": (g, z * 4 + (1 - y) * 2 + x),
        "s": (1 - g, s),
    }
    for k in (1, 2, 3):
        out["z%d" % k] = (g, ((z + k) % 4) * 4 + y * 2 + x)
    return out


def entry_barrier(where):
    sem = pltpu.get_barrier_semaphore()
    names = ("x", "y", "s", "z1", "z2", "z3")
    for name in names:
        pl.semaphore_signal(sem, inc=1, device_id=where[name], device_id_type=MESH)
    pl.semaphore_wait(sem, len(names))


def gather_kernel(routes, look, *refs):
    n = len(routes)
    ins, outs = refs[:n], refs[n : 2 * n]
    send_sem, recv_sem, local_sem = refs[2 * n :]
    g, s, z, y, x = coords()
    where = partners()
    entry_barrier(where)
    both = [r.isupper() for r in routes]
    zs = [z, (z + 1) % 4, (z + 3) % 4, (z + 2) % 4]

    def place(k, dy, dx):
        return (g, zs[k] * 4 + (1 - y if dy else y) * 2 + (1 - x if dx else x))

    def slot(p, who):
        return outs[p].at[who[0], who[1]] if both[p] else outs[p].at[who[1]]

    sends = []
    copies = []

    def send(p, who, to, own=False):
        src = ins[p] if own else slot(p, who)
        copy = pltpu.make_async_remote_copy(
            src,
            slot(p, who),
            send_sem.at[len(sends)],
            recv_sem.at[who[0], who[1], p],
            device_id=where[to],
            device_id_type=MESH,
        )
        copy.start()
        sends.append(copy)

    def wait(p, who):
        ref = slot(p, who)
        pltpu.make_async_remote_copy(
            ref,
            ref,
            send_sem.at[0],
            recv_sem.at[who[0], who[1], p],
            device_id=where["x"],
            device_id_type=MESH,
        ).wait_recv()

    def across(p, who):
        if both[p]:
            send(p, who, "s")

    def own(p):
        copy = pltpu.make_async_copy(ins[p], slot(p, (g, s)), local_sem.at[p])
        copy.start()
        copies.append(copy)
        for to in ("z1", "z3", "z2", "x", "y"):
            send(p, (g, s), to, True)
        if both[p]:
            send(p, (g, s), "s", True)

    def from_z(p):
        for k in (1, 2, 3):
            who = place(k, 0, 0)
            wait(p, who)
            send(p, who, "x")
            send(p, who, "y")
            across(p, who)

    def from_xy(p):
        for k in range(4):
            who = place(k, 0, 1)
            wait(p, who)
            if routes[p] in "Aa":
                send(p, who, "y")
            across(p, who)
            who = place(k, 1, 0)
            wait(p, who)
            if routes[p] in "Bb":
                send(p, who, "x")
            across(p, who)

    def diagonal(p):
        for k in range(4):
            who = place(k, 1, 1)
            wait(p, who)
            across(p, who)

    def from_core(p):
        if both[p]:
            for k in range(4):
                for dy in (0, 1):
                    for dx in (0, 1):
                        wait(p, (1 - g, place(k, dy, dx)[1]))

    for p in range(min(look, n)):
        own(p)
    for t in range(n + 3):
        if t + look < n:
            own(t + look)
        if t < n:
            from_z(t)
        if 0 <= t - 1 < n:
            from_xy(t - 1)
        if 0 <= t - 2 < n:
            diagonal(t - 2)
        if 0 <= t - 3 < n:
            from_core(t - 3)
    for copy in copies:
        copy.wait()
    for copy in sends:
        copy.wait_send()


def gather_call(arrays, routes, look):
    n = len(arrays)
    count = sum(31 if r.isupper() else 15 for r in routes)
    shapes = [
        jax.ShapeDtypeStruct(((2, 16) if r.isupper() else (16,)) + a.shape, a.dtype)
        for a, r in zip(arrays, routes)
    ]
    return pl.pallas_call(
        functools.partial(gather_kernel, routes, look),
        out_shape=shapes,
        in_specs=[ANY] * n,
        out_specs=[ANY] * n,
        scratch_shapes=[
            pltpu.SemaphoreType.DMA((count,)),
            pltpu.SemaphoreType.DMA((2, 16, n)),
            pltpu.SemaphoreType.DMA((n,)),
        ],
        compiler_params=pltpu.CompilerParams(collective_id=1, has_side_effects=True),
        name="gather_weights",
    )(*arrays)


def make_pieces(prompt_parts, rows):
    pieces = []

    def add(src, r0, count, c0, cols, both=True, dtype=BF):
        pieces.append(
            dict(src=src, r0=r0, rows=count, c0=c0, cols=cols, both=both, dtype=dtype)
        )

    for r in range(0, 128, rows):
        add(5, r, rows, 0, 1024)
    for c in range(4):
        for r in range(0, 32, rows):
            add(4, r, rows, c * 1024, 1024)
    for i in (3, 0, 1, 2):
        for r in range(0, 32, rows):
            add(i, r, rows, 0, 1024)
    add(6, 0, 8, 0, 128, True, F32)
    for j in range(prompt_parts):
        add(7 + j, 0, 24, 0, 1024, False)
    scratch = []
    for i, piece in enumerate(pieces):
        piece["order"] = (2, 1, 0) if i % 2 == 0 else (1, 2, 0)
        piece["bufs"] = {}
        tail = (piece["rows"], piece["cols"])

        def buf(name, shape):
            piece["bufs"][name] = len(scratch)
            scratch.append(pltpu.VMEM(shape + tail, piece["dtype"]))

        dims = list(ZYX)
        buf("own", tuple(dims))
        if piece["both"]:
            buf("other", tuple(dims))
        for stage, axis in enumerate(piece["order"]):
            size = dims[axis]
            dims[axis] = 1
            buf("recv%d" % stage, (size - 1,) + tuple(dims))
            if stage < 2:
                buf("sum%d" % stage, tuple(dims))
    return pieces, scratch


def one_along(ref, axis, start):
    index = [slice(None)] * 3
    index[axis] = pl.ds(start, 1)
    return ref.at[tuple(index)]


def scatter_kernel(pieces, n_in, n_out, n_buf, *refs):
    ins, outs = refs[:n_in], refs[n_in : n_in + n_out]
    bufs = refs[n_in + n_out : n_in + n_out + n_buf]
    send_sem, recv_sem, local_sem = refs[n_in + n_out + n_buf :]
    g, s, z, y, x = coords()
    me = (z, y, x)
    where = partners()
    entry_barrier(where)
    pending = []
    n_local = [0]

    def buf(piece, name):
        return bufs[piece["bufs"][name]]

    def push(src, dst, to):
        i = len(pending)
        copy = pltpu.make_async_remote_copy(
            src,
            dst,
            send_sem.at[i],
            recv_sem.at[i],
            device_id=where[to],
            device_id_type=MESH,
        )
        copy.start()
        pending.append(copy)
        return copy

    def window(piece, half):
        ref = ins[piece["src"]]
        index = (slice(None),) * 3 + (
            pl.ds(piece["r0"], piece["rows"]),
            pl.ds(piece["c0"], piece["cols"]),
        )
        return ref.at[(half,) + index] if piece["both"] else ref.at[index]

    def begin(piece):
        if piece["both"]:
            piece["across"] = push(window(piece, 1 - g), buf(piece, "other"), "s")
        copy = pltpu.make_async_copy(
            window(piece, g), buf(piece, "own"), local_sem.at[n_local[0]]
        )
        n_local[0] += 1
        copy.start()
        piece["load"] = copy

    def add_up(reads, dims, write):
        count = dims[0] * dims[1] * dims[2]

        def body(i, carry):
            iz = i // (dims[1] * dims[2])
            rest = i % (dims[1] * dims[2])
            at = (iz, rest // dims[2], rest % dims[2])
            total = None
            for read in reads:
                value = read(*at).astype(F32)
                total = value if total is None else total + value
            write(at, total)
            return carry

        if count == 1:
            body(0, 0)
        else:
            lax.fori_loop(0, count, body, 0)

    def exchange(piece, stage, cur):
        axis = piece["order"][stage]
        recv = buf(piece, "recv%d" % stage)
        if axis == 2:
            got = [push(one_along(cur, 2, 1 - x), recv.at[0], "x")]
        elif axis == 1:
            got = [push(one_along(cur, 1, 1 - y), recv.at[0], "y")]
        else:
            got = [
                push(one_along(cur, 0, (z + k) % 4), recv.at[k - 1], "z%d" % k)
                for k in (1, 3, 2)
            ]
        piece["got%d" % stage] = got

    def first(piece):
        piece["load"].wait()
        own = buf(piece, "own")
        if piece["both"]:
            piece["across"].wait_recv()
            other = buf(piece, "other")

            def write(at, total):
                own[at] = total.astype(own.dtype)

            add_up([lambda *at: own[at], lambda *at: other[at]], ZYX, write)
        piece["dims"] = list(ZYX)
        piece["cur"] = own
        exchange(piece, 0, own)

    def reduce(piece, stage):
        axis = piece["order"][stage]
        for copy in piece["got%d" % stage]:
            copy.wait_recv()
        cur = piece["cur"]
        recv = buf(piece, "recv%d" % stage)
        size = piece["dims"][axis]
        piece["dims"][axis] = 1

        def mine(*at):
            at = list(at)
            at[axis] = me[axis]
            return cur[tuple(at)]

        reads = [mine]
        for j in range(size - 1):
            reads.append(lambda *at, j=j: recv[(j,) + at])
        if stage < 2:
            dst = buf(piece, "sum%d" % stage)

            def write(at, total):
                dst[at] = total.astype(dst.dtype)

            add_up(reads, piece["dims"], write)
            piece["cur"] = dst
            exchange(piece, stage + 1, dst)
        else:
            out = outs[piece["src"]]

            def write(at, total):
                out[
                    pl.ds(piece["r0"], piece["rows"]), pl.ds(piece["c0"], piece["cols"])
                ] = total

            add_up(reads, piece["dims"], write)

    n = len(pieces)
    for piece in pieces:
        begin(piece)
    for t in range(n + 3):
        if t < n:
            first(pieces[t])
        for stage in range(3):
            if 0 <= t - 1 - stage < n:
                reduce(pieces[t - 1 - stage], stage)
    for copy in pending:
        copy.wait_send()


def scatter_call(arrays, out_shapes, prompt_parts, rows):
    pieces, scratch = make_pieces(prompt_parts, rows)
    remote = sum(6 if piece["both"] else 5 for piece in pieces)
    vmem = pl.BlockSpec(memory_space=pltpu.VMEM)
    return pl.pallas_call(
        functools.partial(
            scatter_kernel, pieces, len(arrays), len(out_shapes), len(scratch)
        ),
        out_shape=[jax.ShapeDtypeStruct(shape, F32) for shape in out_shapes],
        in_specs=[ANY] * len(arrays),
        out_specs=[vmem] * len(out_shapes),
        scratch_shapes=scratch
        + [
            pltpu.SemaphoreType.DMA((remote,)),
            pltpu.SemaphoreType.DMA((remote,)),
            pltpu.SemaphoreType.DMA((len(pieces),)),
        ],
        compiler_params=pltpu.CompilerParams(
            collective_id=2, has_side_effects=True, vmem_limit_bytes=60 << 20
        ),
        name="reduce_grads",
    )(*arrays)


def place_rows_kernel(idx_ref, new_ref, old_ref, out_ref):
    length, count = old_ref.shape[1], new_ref.shape[1]
    spot = lax.broadcasted_iota(jnp.int32, (length, count), 0)
    hit = spot == idx_ref[0]
    pick = jnp.where(hit, 1.0, 0.0)
    routed = jnp.sum(pick, axis=1, keepdims=True) > 0.5
    moved = jnp.dot(pick.astype(BF), new_ref[0], preferred_element_type=F32)
    out_ref[0] = jnp.where(routed, moved.astype(BF), old_ref[0])


def place_rows(old, idx, new):
    blocks, length, width = old.shape
    count = idx.shape[1]
    return pl.pallas_call(
        place_rows_kernel,
        out_shape=jax.ShapeDtypeStruct(old.shape, old.dtype),
        grid=(blocks,),
        in_specs=[
            pl.BlockSpec((1, 1, count), lambda b: (b, 0, 0)),
            pl.BlockSpec((1, count, width), lambda b: (b, 0, 0)),
            pl.BlockSpec((1, length, width), lambda b: (b, 0, 0)),
        ],
        out_specs=pl.BlockSpec((1, length, width), lambda b: (b, 0, 0)),
        name="place_rows",
    )(idx[:, None, :], new, old)


def stacked(pair):
    left = lax.broadcasted_iota(jnp.int32, pair.shape, 1) < HD
    zero = jnp.zeros_like(pair)
    return jnp.concatenate([jnp.where(left, pair, zero), jnp.where(left, zero, pair)], 0)


def unstacked(both):
    rows = both.shape[0] // 2
    left = lax.broadcasted_iota(jnp.int32, (rows, both.shape[1]), 1) < HD
    return jnp.where(left, both[:rows], both[rows:])


def dot_nt(a, b):
    return lax.dot_general(a, b, (((1,), (1,)), ((), ())), preferred_element_type=F32)


def dot_tn(a, b):
    return lax.dot_general(a, b, (((0,), (0,)), ((), ())), preferred_element_type=F32)


def probabilities(q2, keys, seen):
    scores = dot_nt(q2, keys) * SCALE
    masked = jnp.where(seen, scores, NEGATIVE)
    raised = jnp.exp(masked - jnp.max(masked, -1, keepdims=True))
    return raised / jnp.sum(raised, -1, keepdims=True)


def seen_cont(meta_row, rows, slots):
    own = (
        lax.broadcasted_iota(jnp.int32, (2 * rows, rows), 1)
        <= lax.broadcasted_iota(jnp.int32, (2 * rows, rows), 0) % rows
    )
    ours = jnp.broadcast_to(meta_row < FAR, (2 * rows, slots))
    return jnp.concatenate([ours.astype(jnp.int32), own.astype(jnp.int32)], 1) > 0


def seen_prompt(meta_row, rank_col):
    return meta_row <= jnp.concatenate([rank_col, rank_col], 0)


def attend_cont_kernel(sel, q_ref, k_ref, v_ref, kp_ref, vp_ref, meta_ref, o_ref):
    rows, slots = q_ref.shape[0], kp_ref.shape[1]
    seen = seen_cont(meta_ref[0], rows, slots)
    for pair in range(q_ref.shape[1] // 128):
        lanes = pl.ds(pair * 128, 128)
        keys = jnp.concatenate([kp_ref[0, :, lanes], k_ref[:, lanes]], 0)
        values = jnp.concatenate([vp_ref[0, :, lanes], v_ref[:, lanes]], 0)
        probs = probabilities(stacked(q_ref[:, lanes]), keys, seen)
        out = jnp.dot(probs.astype(BF), values, preferred_element_type=F32)
        o_ref[:, lanes] = unstacked(out).astype(BF)


def attend_prompt_kernel(sel, q_ref, rank_ref, kp_ref, vp_ref, meta_ref, o_ref):
    seen = seen_prompt(meta_ref[0], rank_ref[0])
    for pair in range(q_ref.shape[1] // 128):
        lanes = pl.ds(pair * 128, 128)
        probs = probabilities(stacked(q_ref[:, lanes]), kp_ref[0, :, lanes], seen)
        out = jnp.dot(probs.astype(BF), vp_ref[0, :, lanes], preferred_element_type=F32)
        o_ref[:, lanes] = unstacked(out).astype(BF)


def score_grads(probs, do2, values):
    grads = dot_nt(do2, values)
    inner = jnp.sum(probs * grads, -1, keepdims=True)
    return (probs * (grads - inner)).astype(BF)


def back_prompt_kernel(
    sel, q_ref, do_ref, rank_ref, kp_ref, vp_ref, meta_ref, dq_ref, dk_ref, dv_ref
):
    seen = seen_prompt(meta_ref[0], rank_ref[0])
    for pair in range(q_ref.shape[1] // 128):
        lanes = pl.ds(pair * 128, 128)
        q2, do2 = stacked(q_ref[:, lanes]), stacked(do_ref[:, lanes])
        keys, values = kp_ref[0, :, lanes], vp_ref[0, :, lanes]
        probs = probabilities(q2, keys, seen)
        ds = score_grads(probs, do2, values)
        dq = jnp.dot(ds, keys, preferred_element_type=F32)
        dq_ref[:, lanes] = (unstacked(dq) * SCALE).astype(BF)
        dk_ref[0, :, lanes] = dot_tn(ds, q2) * SCALE
        dv_ref[0, :, lanes] = dot_tn(probs.astype(BF), do2)


def back_cont_kernel(
    sel,
    sel_prompt,
    q_ref,
    k_ref,
    v_ref,
    do_ref,
    kp_ref,
    vp_ref,
    meta_ref,
    dk_first,
    dv_first,
    dq_ref,
    dk_ref,
    dv_ref,
    dkp_ref,
    dvp_ref,
):
    rows, slots = q_ref.shape[0], kp_ref.shape[1]
    step = pl.program_id(0)

    @pl.when(step == 0)
    def _():
        dkp_ref[...] = jnp.zeros_like(dkp_ref)
        dvp_ref[...] = jnp.zeros_like(dvp_ref)
        for m in range(dk_first.shape[0]):
            dkp_ref[sel_prompt[m]] = dk_first[m]
            dvp_ref[sel_prompt[m]] = dv_first[m]

    which = sel[step]
    seen = seen_cont(meta_ref[0], rows, slots)
    for pair in range(q_ref.shape[1] // 128):
        lanes = pl.ds(pair * 128, 128)
        q2, do2 = stacked(q_ref[:, lanes]), stacked(do_ref[:, lanes])
        keys = jnp.concatenate([kp_ref[0, :, lanes], k_ref[:, lanes]], 0)
        values = jnp.concatenate([vp_ref[0, :, lanes], v_ref[:, lanes]], 0)
        probs = probabilities(q2, keys, seen)
        ds = score_grads(probs, do2, values)
        dq = jnp.dot(ds, keys, preferred_element_type=F32)
        dq_ref[:, lanes] = (unstacked(dq) * SCALE).astype(BF)
        dk = dot_tn(ds, q2) * SCALE
        dv = dot_tn(probs.astype(BF), do2)
        dk_ref[:, lanes] = dk[slots:].astype(BF)
        dv_ref[:, lanes] = dv[slots:].astype(BF)
        dkp_ref[which, :, lanes] += dk[:slots]
        dvp_ref[which, :, lanes] += dv[:slots]


def attention_specs(rows, width, slots):
    row = pl.BlockSpec((rows, width), lambda b, sel, *_: (b, 0))
    slot = pl.BlockSpec((1, slots, width), lambda b, sel, *_: (sel[b], 0, 0))
    meta = pl.BlockSpec((1, 1, slots), lambda b, sel, *_: (sel[b], 0, 0))
    rank = pl.BlockSpec((1, rows, 1), lambda b, sel, *_: (b, 0, 0))
    return row, slot, meta, rank


def attend_cont(sel, q, k, v, kp, vp, meta, rows):
    width, slots = q.shape[1], kp.shape[1]
    row, slot, key, _ = attention_specs(rows, width, slots)
    return pl.pallas_call(
        attend_cont_kernel,
        out_shape=jax.ShapeDtypeStruct(q.shape, BF),
        grid_spec=pltpu.PrefetchScalarGridSpec(
            num_scalar_prefetch=1,
            grid=(q.shape[0] // rows,),
            in_specs=[row, row, row, slot, slot, key],
            out_specs=row,
        ),
        name="attend_cont",
    )(sel, q, k, v, kp, vp, meta)


def attend_prompt(sel, q, rank, kp, vp, meta, rows):
    width, slots = q.shape[1], kp.shape[1]
    row, slot, key, ranks = attention_specs(rows, width, slots)
    return pl.pallas_call(
        attend_prompt_kernel,
        out_shape=jax.ShapeDtypeStruct(q.shape, BF),
        grid_spec=pltpu.PrefetchScalarGridSpec(
            num_scalar_prefetch=1,
            grid=(q.shape[0] // rows,),
            in_specs=[row, ranks, slot, slot, key],
            out_specs=row,
        ),
        name="attend_prompt",
    )(sel, q, rank, kp, vp, meta)


def back_prompt(sel, q, do, rank, kp, vp, meta, rows):
    width, slots = q.shape[1], kp.shape[1]
    row, slot, key, ranks = attention_specs(rows, width, slots)
    parts = q.shape[0] // rows
    part = pl.BlockSpec((1, slots, width), lambda b, sel: (b, 0, 0))
    return pl.pallas_call(
        back_prompt_kernel,
        out_shape=(
            jax.ShapeDtypeStruct(q.shape, BF),
            jax.ShapeDtypeStruct((parts, slots, width), F32),
            jax.ShapeDtypeStruct((parts, slots, width), F32),
        ),
        grid_spec=pltpu.PrefetchScalarGridSpec(
            num_scalar_prefetch=1,
            grid=(parts,),
            in_specs=[row, row, ranks, slot, slot, key],
            out_specs=[row, part, part],
        ),
        name="back_prompt",
    )(sel, q, do, rank, kp, vp, meta)


def back_cont(sel, sel_prompt, q, k, v, do, kp, vp, meta, dk_first, dv_first, rows):
    width, slots = q.shape[1], kp.shape[1]
    row, slot, key, _ = attention_specs(rows, width, slots)
    whole = pl.BlockSpec(memory_space=pltpu.VMEM)
    total = jax.ShapeDtypeStruct(kp.shape, F32)
    return pl.pallas_call(
        back_cont_kernel,
        out_shape=(jax.ShapeDtypeStruct(q.shape, BF),) * 3 + (total, total),
        grid_spec=pltpu.PrefetchScalarGridSpec(
            num_scalar_prefetch=2,
            grid=(q.shape[0] // rows,),
            in_specs=[row, row, row, row, slot, slot, key, whole, whole],
            out_specs=[row, row, row, whole, whole],
        ),
        compiler_params=pltpu.CompilerParams(vmem_limit_bytes=56 << 20),
        name="back_cont",
    )(sel, sel_prompt, q, k, v, do, kp, vp, meta, dk_first, dv_first)


def matmul(a, b):
    return jnp.dot(a, b, preferred_element_type=F32)


def matmul_nt(a, b):
    return jnp.einsum("qd,ad->qa", a, b, preferred_element_type=F32)


def matmul_tn(a, b):
    return jnp.einsum("qa,qd->ad", a, b, preferred_element_type=F32)


def scale_of(rows):
    return lax.rsqrt(jnp.mean(rows * rows, -1, keepdims=True) + EPS)


def norm_back(grad, rows, scale, gain):
    moved = gain * grad
    return scale * moved - rows * (scale * scale * scale) * jnp.mean(
        rows * moved, -1, keepdims=True
    )


def gelu_parts(u):
    t = jnp.tanh(ROOT * (u + 0.044715 * u * u * u))
    value = 0.5 * u * (1.0 + t)
    slope = 0.5 * (1.0 + t) + 0.5 * u * (1.0 - t * t) * ROOT * (1.0 + 3.0 * 0.044715 * u * u)
    return value, slope


def slot_table(routes, seq_count, p_dev, pcap):
    prompt_len = p_dev * seq_count // 2
    routed_len = routes.shape[1]
    owners = jnp.arange(seq_count, dtype=jnp.int32)
    owner_prompt = owners // (seq_count // 2)
    owner_base = owners * p_dev - owner_prompt * prompt_len
    owner_routes = routes[owner_prompt]
    below = jnp.sum((owner_routes < owner_base[:, None]).astype(jnp.int32), 1)
    inside = jnp.sum((owner_routes < (owner_base + p_dev)[:, None]).astype(jnp.int32), 1) - below
    slot_ids = jnp.arange(pcap, dtype=jnp.int32)
    slot_rank = below[:, None] + slot_ids[None, :]
    slot_valid = slot_ids[None, :] < inside[:, None]
    picked = jnp.take_along_axis(owner_routes, jnp.clip(slot_rank, 0, routed_len - 1), 1)
    places = jnp.clip(picked - owner_base[:, None], 0, p_dev - 1)
    return slot_rank, slot_valid, places


def pad_rows(rows, count):
    return jnp.pad(rows, ((0, 0), (0, count - rows.shape[1]), (0, 0)))


def part(weights, gains, chunk, slots_x):
    w_query, w_key, w_value, w_out, w_up, w_down = weights
    gain_attn, gain_mlp, router_bf = gains
    router = router_bf.astype(F32)
    n_cont = chunk["xc"].shape[0]
    width = chunk["xc"].shape[1]
    routed = chunk["routed"]
    x_bf = jnp.concatenate([chunk["xc"], chunk["xp"]], 0)
    x = x_bf.astype(F32)
    c1 = scale_of(x)
    n1 = (x * c1 * gain_attn).astype(BF)
    xs = slots_x.reshape(-1, width).astype(F32)
    cs = scale_of(xs)
    ns = (xs * cs * gain_attn).astype(BF)
    n_kv = jnp.concatenate([n1[:n_cont], ns], 0)
    q = matmul(n1, w_query).astype(BF)
    k = matmul(n_kv, w_key).astype(BF)
    v = matmul(n_kv, w_value).astype(BF)
    q_c, q_p = q[:n_cont], q[n_cont:]
    k_c, v_c = k[:n_cont], v[:n_cont]
    meta = chunk["meta"]
    slots = meta.shape[2]
    k_s = k[n_cont:].reshape(-1, slots, width)
    v_s = v[n_cont:].reshape(-1, slots, width)
    sel, sel_prompt, rank = chunk["sel"], chunk["sel_prompt"], chunk["rank"]
    o_c = attend_cont(sel, q_c, k_c, v_c, k_s, v_s, meta, routed)
    o_p = attend_prompt(sel_prompt, q_p, rank, k_s, v_s, meta, PPAD)
    o = jnp.concatenate([o_c, o_p], 0)
    a = matmul(o, w_out)
    h = x + a
    c2 = scale_of(h)
    n2 = (h * c2 * gain_mlp).astype(BF)
    u = matmul(n2, w_up)
    value, slope = gelu_parts(u)
    g = value.astype(BF)
    m = matmul(g, w_down)
    r = 1.0 / (1.0 + jnp.exp(-matmul(x_bf, router_bf[:, None])))
    both = a + m
    y = (x + r * both).astype(BF)

    dy = jnp.concatenate([chunk["dyc"], chunk["dyp"]], 0).astype(F32)
    dz = jnp.sum(dy * both, -1, keepdims=True) * r * (1.0 - r)
    router_grad = jnp.sum(dz * x, 0)
    dx1 = dy + dz * router
    dbranch = dy * r
    dm = dbranch.astype(BF)
    down_grad = matmul_tn(g, dm)
    du = (matmul_nt(dm, w_down) * slope).astype(BF)
    up_grad = matmul_tn(n2, du)
    dn2 = matmul_nt(du, w_up)
    dh = norm_back(dn2, h, c2, gain_mlp)
    gain_mlp_grad = jnp.sum(dn2 * h * c2, 0)
    da = (dbranch + dh).astype(BF)
    out_grad = matmul_tn(o, da)
    do = matmul_nt(da, w_out).astype(BF)
    dq_p, dk_first, dv_first = back_prompt(
        sel_prompt, q_p, do[n_cont:], rank, k_s, v_s, meta, PPAD
    )
    dq_c, dk_c, dv_c, dk_s, dv_s = back_cont(
        sel, sel_prompt, q_c, k_c, v_c, do[:n_cont], k_s, v_s, meta, dk_first, dv_first, routed
    )
    dq = jnp.concatenate([dq_c, dq_p], 0)
    dk = jnp.concatenate([dk_c, dk_s.reshape(-1, width).astype(BF)], 0)
    dv = jnp.concatenate([dv_c, dv_s.reshape(-1, width).astype(BF)], 0)
    query_grad = matmul_tn(n1, dq)
    key_grad = matmul_tn(n_kv, dk)
    value_grad = matmul_tn(n_kv, dv)
    dn_q = matmul_nt(dq, w_query)
    dn_kv = matmul_nt(dk, w_key) + matmul_nt(dv, w_value)
    dn_c = dn_q[:n_cont] + dn_kv[:n_cont]
    dn_p, dn_s = dn_q[n_cont:], dn_kv[n_cont:]
    gain_attn_grad = (
        jnp.sum(dn_c * x[:n_cont] * c1[:n_cont], 0)
        + jnp.sum(dn_p * x[n_cont:] * c1[n_cont:], 0)
        + jnp.sum(dn_s * xs * cs, 0)
    )
    dx_rest = dx1 + dh
    dx_c = (
        dx_rest[:n_cont] + norm_back(dn_c, x[:n_cont], c1[:n_cont], gain_attn)
    ).astype(BF)
    grads = (query_grad, key_grad, value_grad, out_grad, up_grad, down_grad)
    small = (gain_attn_grad, gain_mlp_grad, router_grad)
    tail = (dn_p, dx_rest[n_cont:], x[n_cont:], c1[n_cont:])
    return y, dx_c, grads, small, dn_s, tail


def finish_prompt(tail, received, gain_attn, pcap):
    dn_p, rest, x, c1 = tail
    width = x.shape[1]
    count = received.shape[0]
    dn = dn_p + pad_rows(received, PPAD).reshape(-1, width)
    dx = (rest + norm_back(dn, x, c1, gain_attn)).astype(BF)
    return dx.reshape(count, PPAD, width)


def body(
    prompt_x,
    cont_x,
    prompt_routes,
    cont_routes,
    cont_group,
    w_query,
    w_key,
    w_value,
    w_out,
    w_up,
    w_down,
    gain_attn,
    gain_mlp,
    w_router,
    prompt_cot,
    cont_cot,
):
    seq_count = lax.axis_size("seq")
    grp_count = lax.axis_size("grp")
    tuned = seq_count == 16 and grp_count == 2
    seq_index = lax.axis_index("seq")
    micro, p_dev, width = prompt_x.shape[0], prompt_x.shape[2], prompt_x.shape[3]
    conts, length, routed = cont_x.shape[2], cont_x.shape[3], cont_routes.shape[3]
    pcap = 3 * p_dev // 16
    own_prompt = seq_index // (seq_count // 2)
    group = 2 if micro % 2 == 0 else 1
    shards = (w_query, w_key, w_value, w_out, w_up, w_down)

    tables = [slot_table(prompt_routes[m, 0], seq_count, p_dev, pcap) for m in range(micro)]
    metas, ranks, places, rows_p, dys_p = [], [], [], [], []
    for m in range(micro):
        slot_rank, slot_valid, slot_places = tables[m]
        metas.append(jnp.where(slot_valid, slot_rank, FAR).reshape(2, 1, -1))
        pick = lambda t: lax.dynamic_index_in_dim(t, seq_index, 0, keepdims=False)
        valid, rank, place = pick(slot_valid), pick(slot_rank), pick(slot_places)
        ranks.append(jnp.pad(jnp.where(valid, rank, -1), (0, PPAD - pcap), constant_values=-1))
        places.append(jnp.pad(jnp.where(valid, place, -1), (0, PPAD - pcap), constant_values=-1))
        rows_p.append(jnp.take(prompt_x[m, 0], place, axis=0))
        dy = jnp.take(prompt_cot[m, 0], place, axis=0)
        dys_p.append(jnp.where(valid[:, None], dy, jnp.zeros_like(dy)))
    places = jnp.stack(places)
    xc = jnp.take_along_axis(cont_x[:, 0], cont_routes[:, 0, :, :, None], 2)
    dyc = jnp.take_along_axis(cont_cot[:, 0], cont_routes[:, 0, :, :, None], 2)

    if tuned:
        tiny = jnp.pad(
            jnp.concatenate([gain_attn, gain_mlp, w_router])[None, :], ((0, 7), (0, 32))
        )
        up4 = w_up.reshape(4, 8, -1)
        down4 = w_down.reshape(4, -1, width)
        arrays = rows_p + [tiny, w_query, w_key, w_value, w_out]
        routes = "ab" * (micro // 2) + "a" * (micro % 2) + "ABABA"
        arrays += [w_up, w_down]
        routes += "BA"
        got = gather_call(arrays, routes, 5)
        slots_x = jnp.stack(got[:micro])
        tiny = got[micro].reshape(32, 8, 128)
        vectors = tuple(tiny[:, 0, 32 * i : 32 * i + 32].reshape(-1) for i in range(3))
        weights = tuple(t.reshape(-1, t.shape[-1]) for t in got[micro + 1 :])
    else:
        gather = lambda t: lax.all_gather(t, ("grp", "seq"), axis=0, tiled=True)
        slots_x = lax.all_gather(jnp.stack(rows_p), "seq", axis=1, tiled=False)
        weights = tuple(gather(t) for t in shards)
        vectors = tuple(gather(t) for t in (gain_attn, gain_mlp, w_router))
    gains = (vectors[0].astype(F32), vectors[1].astype(F32), vectors[2])
    slots_x = slots_x.reshape(micro, 2, -1, width)

    totals = None
    ys, dxs, slot_grads, tails = [], [], [], []
    for start in range(0, micro, group):
        mine = slice(start, start + group)
        sel = (
            jnp.arange(group, dtype=jnp.int32)[:, None] * 2 + cont_group[mine, 0]
        ).reshape(-1)
        chunk = dict(
            routed=routed,
            xc=xc[mine].reshape(-1, width),
            xp=pad_rows(jnp.stack(rows_p[mine]), PPAD).reshape(-1, width),
            dyc=dyc[mine].reshape(-1, width),
            dyp=pad_rows(jnp.stack(dys_p[mine]), PPAD).reshape(-1, width),
            meta=jnp.concatenate(metas[mine], 0),
            rank=jnp.stack(ranks[mine])[:, :, None],
            sel=sel,
            sel_prompt=jnp.arange(group, dtype=jnp.int32) * 2 + own_prompt,
        )
        y, dx_c, grads, small, dn_s, tail = part(weights, gains, chunk, slots_x[mine])
        ys.append(y)
        dxs.append(dx_c)
        slot_grads.append(dn_s.astype(BF).reshape(group, seq_count, pcap, width))
        tails.append(tail)
        new = tuple(grads) + tuple(small)
        totals = new if totals is None else tuple(a + b for a, b in zip(totals, new))

    if tuned:
        split = lambda t: t.astype(BF).reshape((2,) + ZYX + (-1, t.shape[-1]))
        small = jnp.concatenate([t.reshape(32, 1, 32) for t in totals[6:]], 2)
        small = jnp.pad(small, ((0, 0), (0, 7), (0, 32))).reshape((2,) + ZYX + (8, 128))
        slot_list = [slot_grads[m // group][m % group] for m in range(micro)]
        arrays = [split(t) for t in totals[:6]] + [small]
        arrays += [t.reshape(ZYX + (pcap, width)) for t in slot_list]
        shapes = [t.shape for t in shards] + [(8, 128)] + [(pcap, width)] * micro
        out = scatter_call(arrays, shapes, micro, 32)
        final = tuple(out[:6]) + tuple(out[6][0, 32 * i : 32 * i + 32] for i in range(3))
        received = jnp.stack(out[7:])
    else:
        final = tuple(
            lax.psum_scatter(t, ("grp", "seq"), scatter_dimension=0, tiled=True) for t in totals
        )
        received = lax.psum_scatter(
            jnp.concatenate(slot_grads, 0), "seq", scatter_dimension=1, tiled=False
        ).astype(F32)

    y_c = jnp.concatenate([t[: group * conts * routed] for t in ys], 0)
    y_p = jnp.concatenate([t[group * conts * routed :] for t in ys], 0)
    dx_c = jnp.concatenate(dxs, 0)
    dx_p = jnp.concatenate(
        [
            finish_prompt(tail, received[i * group : (i + 1) * group], gains[0], pcap)
            for i, tail in enumerate(tails)
        ],
        0,
    )
    flat = lambda t: t.reshape((-1,) + t.shape[-2:])
    rows_of = lambda t: t.reshape(-1, routed, width)
    idx_c = cont_routes.reshape(-1, routed)
    prompt_out = place_rows(flat(prompt_x), places, y_p.reshape(-1, PPAD, width))
    cont_out = place_rows(flat(cont_x), idx_c, rows_of(y_c))
    cont_grad = place_rows(flat(cont_cot), idx_c, rows_of(dx_c))
    prompt_grad = place_rows(flat(prompt_cot), places, dx_p)
    return (
        prompt_out.reshape(prompt_x.shape),
        cont_out.reshape(cont_x.shape),
        prompt_grad.reshape(prompt_x.shape),
        cont_grad.reshape(cont_x.shape),
    ) + final


def solution(mesh):
    both = ("grp", "seq")
    in_specs = (
        P(None, "grp", "seq", None),
        P(None, "grp", "seq", None, None),
        P(None, "grp", None, None),
        P(None, "grp", "seq", None),
        P(None, "grp", "seq"),
    )
    in_specs += (P(both, None),) * 6 + (P(both),) * 3
    in_specs += (P(None, "grp", "seq", None), P(None, "grp", "seq", None, None))
    out_specs = (
        P(None, "grp", "seq", None),
        P(None, "grp", "seq", None, None),
        P(None, "grp", "seq", None),
        P(None, "grp", "seq", None, None),
    )
    out_specs += (P(both, None),) * 6 + (P(both),) * 3
    return jax.shard_map(body, mesh=mesh, in_specs=in_specs, out_specs=out_specs, check_vma=False)
```

time: 2200 us -> 601 us (0.27)
  waiting for transfers between devices: 1550 us -> 0 us
  Pallas kernels: 0 us -> 374 us
  local copies, waits for them, and re-layouts: 241 us -> 61.9 us
  matrix products: 238 us -> 111 us
  blocking collectives: 82.9 us -> 0 us
    reduce_scatter x6 -> x0, waiting for transfers between devices: 1010 us -> none  [the longest x1 363 us: body(): lax.psum_scatter(totals[4], ('grp', 'seq'), scatter_dimension=0, tiled=True)]
    pallas_call x0 -> x10, Pallas kernels: none -> 374 us  [the longest x1 148 us: scatter_call(): pl.pallas_call(functools.partial(scatter_kernel, pieces, len(arrays), len...]
    all_gather x8 -> x0, waiting for transfers between devices: 332 us -> none  [the longest x2 109 us: body(): kv_all = lax.all_gather(kv_own, 'seq', axis=0, tiled=True)]
    unnamed x18 -> x0, waiting for transfers between devices: 205 us -> none
    scatter x8 -> x0, local copies, waits for them, and re-layouts: 150 us -> none  [the longest x2 72.8 us: body(): cont_local.at[cont_rows_idx, cont_index]]
    dot_general x50 -> x19, matrix products: 218 us -> 111 us  [the longest x7 39.6 us: matmul(): return jnp.dot(a, b, preferred_element_type=F32)]
    unnamed x2 -> x0, blocking collectives: 82.9 us -> none
  transfers between devices with their start and end apart: 16 -> 0, of which waited for: 13 -> 0; matrix products, arithmetic and copies ran while one was open for 20% -> 0% of each run, Pallas kernels for 0% -> 0%
where the time goes in v1:
time: 601 us; the launch traced here: 590 us
  Pallas kernels  374 us (62%)
  matrix products  111 us (18%)
  local copies, waits for them, and re-layouts  61.9 us (10%)
  other arithmetic  41 us (7%)
    pallas_call x1, Pallas kernels, scatter_call(): pl.pallas_call(functools.partial(scatter_kernel, pieces, len(arrays), len...  148 us
    pallas_call x1, Pallas kernels, gather_call(): pl.pallas_call(functools.partial(gather_kernel, routes, look), out_shape=...  130 us
    dot_general x7, matrix products, matmul(): return jnp.dot(a, b, preferred_element_type=F32)  39.6 us
    pallas_call x1, Pallas kernels, back_cont(): pl.pallas_call(back_cont_kernel, out_shape=(jax.ShapeDtypeStruct(q.shape,...  39 us
    dot_general x6, matrix products, matmul_tn(): return jnp.einsum('qa,qd->ad', a, b, preferred_element_type=F32)  37.5 us
    dot_general x6, matrix products, matmul_nt(): return jnp.einsum('qd,ad->qa', a, b, preferred_element_type=F32)  33.7 us
    pallas_call x4, Pallas kernels, place_rows(): pl.pallas_call(place_rows_kernel, out_shape=jax.ShapeDtypeStruct(old.shap...  25.6 us
    unnamed x153, local copies, waits for them, and re-layouts  14.5 us

profile of v1, /device:TPU:0, one launch (start us, length us, event | category | flops | bytes accessed | tf_op | source)
XLA Modules:
  0.0 590.2 jit_solution(14462931002811779903)
XLA Ops:
  3.5 2.8 gather_fusion.2
  7.9 2.8 gather_fusion.3
  21.1 130.0 %gather_weights.1 = (bf16[16,24,1024]{2,1,0:T(8,128)(2,1)}, bf16[16,24,1024]{2,1,0:T(8,128)(2,1)}, bf16[2,16,8,128]{3,2,1,0:T(8,128)(2,1)}, bf16[2,16,32,1024]{3...) custom-call(bf16[24,1024]{1,0:T(8,128)(2,1)} %get-tuple-element.135., ...), custom_call_target="tpu_custom_call" | custom-call | tf_op jit(solution)/shard_map/gather_weights/pallas_call | solution.py:166
  154.1 3.0 fusion.9
  157.2 7.0 %gather_fusion.4 = bf16[512,1024]{1,0:T(8,128)(2,1)S(1)} fusion(bf16[2,4,512,1024]{3,2,1,0:T(8,128)(2,1)} %bitcast.204, s32[512]{0:T(512)S(1)} %reshape.667), kind=kCustom, calls=%fused_computation.1.clone | custom fusion | bytes 2103296 | tf_op jit(solution)/shard_map/jit(take_along_axis)/gather | solution.py:823
  164.2 7.2 %gather_fusion.7 = bf16[512,1024]{1,0:T(8,128)(2,1)S(1)} fusion(bf16[2,4,512,1024]{3,2,1,0:T(8,128)(2,1)} %bitcast.202, s32[512]{0:T(512)S(1)} %reshape.667), kind=kCustom, calls=%fused_computation.4.clone | custom fusion | bytes 2103296 | tf_op jit(solution)/shard_map/jit(take_along_axis)/gather | solution.py:824
  175.8 3.9 convolution_convert_fusion.2
  182.1 3.9 convolution_convert_fusion.3
  194.5 12.0 %attend_cont.1 = bf16[512,1024]{1,0:T(8,128)(2,1)} custom-call(s32[8]{0:T(128)} %add.266.sel, bf16[512,1024]{1,0:T(8,128)(2,1)} %slice.178.q_ref, bf16[512,1024]{1,0:T(8,128)(2,1)} %slice.180.k_ref, bf16[512,1024]{1,0:T(8,128)(2,1)} %slice.181.v_ref, bf16[4,192,1024]{2,1,0:T(8,128)(2,1)} %bitcast.198, bf16[4,192,1024]{2,1,0:T(8,128)(2,1)} %bitcast.194, ...), custom_call_target="tpu_custom_call" | custom-call | tf_op jit(solution)/shard_map/attend_cont/pallas_call | solution.py:565
  210.4 8.3 %attend_prompt.1 = bf16[64,1024]{1,0:T(8,128)(2,1)} custom-call(s32[2]{0:T(128)} %broadcast_add_fusion.sel.sel_prompt, bf16[64,1024]{1,0:T(8,128)(2,1)} %slice.184.q_ref, s32[2,32,1]{2,1,0:T(8,128)} %copy.38.rank_ref, bf16[4,192,1024]{2,1,0:T(8,128)(2,1)} %bitcast.199, bf16[4,192,1024]{2,1,0:T(8,128)(2,1)} %bitcast.195, s32[4,1,192]{2,1,0:T(1,128)} %pad_add_fusion.meta_ref), custom_call_target="tpu_custom_call" | custom-call | tf_op jit(solution)/shard_map/attend_prompt/pallas_call | solution.py:581
  218.7 5.3 multiply_reduce_fusion.2
  224.7 10.7 %fusion.53 = f32[576,4096]{1,0:T(8,128)} fusion(bf16[1024,4096]{1,0:T(8,128)(2,1)} %bitcast.271, f32[576,1024]{1,0:T(8,128)} %get-tuple-element.107, f32[1024]{0:T(1024)S(1)} %reshape.570, f32[576]{0:T(1024)S(1)} %get-tuple-element.127), kind=kOutput, calls=%fused_computation.203 | convolution fusion | flops 4833607680 | bytes 20191488 | tf_op jit(solution)/shard_map/dot_general | solution.py:636
  237.0 13.9 %fusion.20 = (f32[576]{0:T(1024)S(1)}, bf16[576,1024]{1,0:T(8,128)(2,1)}) fusion(bf16[64,1024]{1,0:T(8,128)(2,1)S(1)} %bitcast.255, bf16[512,1024]{1,0:T(8,128)(2,1)S(1)} %bitcast.227, f32[576]{0:T(1024)S(1)} %add_divide_fusion, bf16[64,1024]{1,0:T(8,128)(2,1)S(1)} %bitcast.235, bf16[512,1024]{1,0:T(8,128)(2,1)S(1)} %bitcast.210, ...), kind=kOutput, calls=%fused_computation.53 | convolution fusion | flops 4861328896 | bytes 23728640 | tf_op jit(solution)/shard_map/dot_general | solution.py:636
  251.5 15.4 %fusion.6 = bf16[576,4096]{1,0:T(8,128)(2,1)} fusion(f32[576,4096]{1,0:T(8,128)} %fusion.53, bf16[4096,1024]{1,0:T(8,128)(2,1)} %bitcast.276, f32[576]{0:T(1024)S(1)} %add_divide_fusion, bf16[64,1024]{1,0:T(8,128)(2,1)S(1)} %bitcast.256, bf16[512,1024]{1,0:T(8,128)(2,1)S(1)} %bitcast.228), kind=kOutput, calls=%fused_computation.18 | convolution fusion | flops 4880203776 | bytes 23726336 | tf_op jit(solution)/shard_map/qd,ad->qa/dot_general | solution.py:640
  267.0 9.6 %multiply_reduce_fusion = (f32[1024]{0:T(1024)}, f32[576]{0:T(1024)S(1)}, f32[576,1024]{1,0:T(8,128)}) fusion(f32[576,1024]{1,0:T(8,128)S(1)} %copy-done.10, f32[576]{0:T(1024)S(1)} %get-tuple-element.127, f32[1024]{0:T(1024)S(1)} %reshape.570, bf16[576,4096]{1,0:T(8,128)(2,1)} %fusion.6, bf16[1024,4096]{1,0:T(8,128)(2,1)S(1)} %bitcast.274), kind=kOutput, calls=%fused_computation.55 | convolution fusion | flops 4835375616 | bytes 17838592 | tf_op jit(solution)/shard_map/qd,ad->qa/dot_general | solution.py:640
  277.3 5.4 fusion.14
  284.8 11.1 %back_prompt.1 = (bf16[64,1024]{1,0:T(8,128)(2,1)}, f32[2,192,1024]{2,1,0:T(8,128)}, f32[2,192,1024]{2,1,0:T(8,128)}) custom-call(s32[2]{0:T(128)} %broadcast_add_fusion.sel.sel_prompt, bf16[64,1024]{1,0:T(8,128)(2,1)} %slice.184.q_ref, bf16[64,1024]{1,0:T(8,128)(2,1)} %slice.190.do_ref, s32[2,32,1]{2,1,0:T(8,128)} %copy.38.rank_ref, ...), custom_call_target="tpu_custom_call" | custom-call | tf_op jit(solution)/shard_map/back_prompt/pallas_call | solution.py:599
  297.0 39.0 %back_cont.1 = (bf16[512,1024]{1,0:T(8,128)(2,1)}, bf16[512,1024]{1,0:T(8,128)(2,1)}, bf16[512,1024]{1,0:T(8,128)(2,1)}, f32[4,192,1024]{2,1,0:T(8,128)}, f32[4,192,1024]{2,1,0:T(8,128)}) custom-call(s32[8]{0:T(128)} %add.266.sel, s32[2]{0:T(128)} %broadcast_add_fusion.sel.sel_prompt, bf16[512,1024]{1,0:T(8,128)(2,1)} %slice.178.q_ref, ...), custom_call_target="tpu_custom_call" | custom-call | tf_op jit(solution)/shard_map/back_cont/pallas_call | solution.py:621
  336.1 2.3 convert_element_type.165
  338.9 2.9 fusion.23
  344.2 2.9 convolution_add_fusion
  347.3 3.0 copy-done.57
  356.0 10.6 %place_rows.7 = bf16[8,512,1024]{2,1,0:T(8,128)(2,1)} custom-call(s32[8,1,64]{2,1,0:T(1,128)} %bitcast.263, bf16[8,64,1024]{2,1,0:T(8,128)(2,1)} %bitcast.225, bf16[8,512,1024]{2,1,0:T(8,128)(2,1)} %bitcast.203), custom_call_target="tpu_custom_call" | custom-call | tf_op jit(solution)/shard_map/place_rows/pallas_call | solution.py:409
  371.1 2.4 fusion.11
  374.6 12.2 %convolution_convert_fusion = bf16[1024,4096]{1,0:T(8,128)(2,1)} fusion(bf16[576,4096]{1,0:T(8,128)(2,1)} %fusion.6, f32[576,1024]{1,0:T(8,128)} %get-tuple-element.107, f32[1024]{0:T(1024)} %copy-done.43, f32[576]{0:T(1024)S(1)} %copy-done.42), kind=kOutput, calls=%fused_computation.20 | convolution fusion | flops 4837801984 | bytes 15472896 | tf_op jit(solution)/shard_map/qa,qd->ad/dot_general | solution.py:644
  386.9 3.1 convolution_convert_fusion.6
  390.1 4.2 convolution_convert_fusion.4
  394.4 4.1 convolution_convert_fusion.5
  398.6 10.6 %convolution_convert_fusion.1 = bf16[4096,1024]{1,0:T(8,128)(2,1)} fusion(f32[576]{0:T(1024)S(1)} %copy-done.46, bf16[64,1024]{1,0:T(8,128)(2,1)S(1)} %bitcast.258, bf16[512,1024]{1,0:T(8,128)(2,1)S(1)} %bitcast.230, f32[576,4096]{1,0:T(8,128)S(1)} %bitcast.286), kind=kOutput, calls=%fused_computation.21 | convolution fusion | flops 4860805120 | bytes 19007744 | tf_op jit(solution)/shard_map/qa,qd->ad/dot_general | solution.py:644
  409.2 3.2 convolution_convert_fusion.7
  412.4 148.2 %reduce_grads.1 = (f32[32,1024]{1,0:T(8,128)}, f32[32,1024]{1,0:T(8,128)}, f32[32,1024]{1,0:T(8,128)}, f32[32,1024]{1,0:T(8,128)}, f32[32,4096]{1,0:T(8,128)}, /...) custom-call(bf16[2,4,2,2,32,1024]{5,4,3,2,1,0:T(8,128)(2,1)} %bitcast.243, ...), custom_call_target="tpu_custom_call" | custom-call | tf_op jit(solution)/shard_map/reduce_grads/pallas_call | solution.py:376
  571.0 10.7 %place_rows.5 = bf16[8,512,1024]{2,1,0:T(8,128)(2,1)} custom-call(s32[8,1,64]{2,1,0:T(1,128)} %bitcast.264, bf16[8,64,1024]{2,1,0:T(8,128)(2,1)} %bitcast.226, bf16[8,512,1024]{2,1,0:T(8,128)(2,1)} %bitcast.205), custom_call_target="tpu_custom_call" | custom-call | tf_op jit(solution)/shard_map/place_rows/pallas_call | solution.py:409
  (288 shorter events, 76.0 us)
Async XLA Ops:
  7.9 7.3 %copy-start.12 = (bf16[2,1,128,1024]{3,2,1,0:T(8,128)(2,1)S(1)}, bf16[2,1,128,1024]{3,2,1,0:T(8,128)(2,1)}, u32[]{:S(2)}) copy-start(bf16[2,1,128,1024]{3,2,1,0:T(8,128)(2,1)} %param.22) | copy-start | bytes 1572868
  7.9 7.9 %copy-start.11 = (bf16[2,1,128,1024]{3,2,1,0:T(8,128)(2,1)S(1)}, bf16[2,1,128,1024]{3,2,1,0:T(8,128)(2,1)}, u32[]{:S(2)}) copy-start(bf16[2,1,128,1024]{3,2,1,0:T(8,128)(2,1)} %param.36) | copy-start | bytes 1572868
  10.7 9.8 %copy-start.51 = (bf16[32]{0:T(256)(128)(2,1)S(1)}, bf16[32]{0:T(256)(128)(2,1)}, u32[]{:S(2)}) copy-start(bf16[32]{0:T(256)(128)(2,1)} %param.35) | copy-start | bytes 196
  10.7 9.7 %copy-start.52 = (bf16[32]{0:T(256)(128)(2,1)S(1)}, bf16[32]{0:T(256)(128)(2,1)}, u32[]{:S(2)}) copy-start(bf16[32]{0:T(256)(128)(2,1)} %param.34) | copy-start | bytes 196
  10.7 9.7 %copy-start.53 = (bf16[32]{0:T(256)(128)(2,1)S(1)}, bf16[32]{0:T(256)(128)(2,1)}, u32[]{:S(2)}) copy-start(bf16[32]{0:T(256)(128)(2,1)} %param.33) | copy-start | bytes 196
  151.1 6.0 %copy-start.32 = (bf16[24,1024]{1,0:T(8,128)(2,1)S(1)}, bf16[24,1024]{1,0:T(8,128)(2,1)}, u32[]{:S(2)}) copy-start(bf16[24,1024]{1,0:T(8,128)(2,1)} %get-tuple-element.135.refs_0_) | copy-start | bytes 147460
  151.1 6.0 %copy-start.40 = (s32[2,1,4,64]{3,2,1,0:T(4,128)S(1)}, s32[2,1,4,64]{3,2,1,0:T(4,128)}, u32[]{:S(2)}) copy-start(s32[2,1,4,64]{3,2,1,0:T(4,128)} %param.25) | copy-start | bytes 6148
  173.3 15.0 %copy-start.5 = (bf16[576,1024]{1,0:T(8,128)(2,1)}, bf16[576,1024]{1,0:T(8,128)(2,1)S(1)}, u32[]{:S(2)}) copy-start(bf16[576,1024]{1,0:T(8,128)(2,1)S(1)} %fusion.17) | copy-start | bytes 3538948
  173.4 8.7 %copy-start.23 = (bf16[512,1024]{1,0:T(8,128)(2,1)}, bf16[512,1024]{1,0:T(8,128)(2,1)S(1)}, u32[]{:S(2)}) copy-start(bf16[512,1024]{1,0:T(8,128)(2,1)S(1)} %slice.179) | copy-start | bytes 3145732
  206.5 12.2 %copy-start.21 = (bf16[512,1024]{1,0:T(8,128)(2,1)S(1)}, bf16[512,1024]{1,0:T(8,128)(2,1)}, u32[]{:S(2)}) copy-start(bf16[512,1024]{1,0:T(8,128)(2,1)} %attend_cont.1) | copy-start | bytes 3145732
  224.6 52.6 %copy-start.41 = (f32[576]{0:T(1024)}, f32[576]{0:T(1024)S(1)}, u32[]{:S(2)}) copy-start(f32[576]{0:T(1024)S(1)} %get-tuple-element.127) | copy-start | bytes 6916
  224.7 42.2 %copy-start.43 = (f32[1024]{0:T(1024)}, f32[1024]{0:T(1024)S(1)}, u32[]{:S(2)}) copy-start(f32[1024]{0:T(1024)S(1)} %reshape.570) | copy-start | bytes 12292
  224.7 12.2 %copy-start.7 = (bf16[2,4,64,1024]{3,2,1,0:T(8,128)(2,1)S(1)}, bf16[2,4,64,1024]{3,2,1,0:T(8,128)(2,1)}, u32[]{:S(2)}) copy-start(bf16[2,4,64,1024]{3,2,1,0:T(8,128)(2,1)} %get-tuple-element.130) | copy-start | bytes 3145732
  236.9 14.6 %copy-start.45 = (f32[576]{0:T(1024)}, f32[576]{0:T(1024)S(1)}, u32[]{:S(2)}) copy-start(f32[576]{0:T(1024)S(1)} %add_divide_fusion) | copy-start | bytes 6916
  236.9 40.3 %copy-start.30 = (bf16[2,32,1024]{2,1,0:T(8,128)(2,1)}, bf16[2,32,1024]{2,1,0:T(8,128)(2,1)S(1)}, u32[]{:S(2)}) copy-start(bf16[2,32,1024]{2,1,0:T(8,128)(2,1)S(1)} %fusion.34) | copy-start | bytes 393220
  237.0 30.0 %slice-start = ((s8[8388608]{0:T(1024)(128)(4,1)}), s8[4194304]{0:T(1024)(128)(4,1)S(1)}, s32[]{:S(2)}) async-start(s8[8388608]{0:T(1024)(128)(4,1)} %bitcast.272), calls=%async_computation | async-start | bytes 8388608
  251.5 15.4 %copy-start.10 = (f32[576,1024]{1,0:T(8,128)S(1)}, f32[576,1024]{1,0:T(8,128)}, u32[]{:S(2)}) copy-start(f32[576,1024]{1,0:T(8,128)} %get-tuple-element.107) | copy-start | bytes 7077892
  251.5 15.5 %slice-start.1 = ((s8[8388608]{0:T(1024)(128)(4,1)}), s8[4194304]{0:T(1024)(128)(4,1)S(1)}, s32[]{:S(2)}) async-start(s8[8388608]{0:T(1024)(128)(4,1)} %bitcast.272), calls=%async_computation.1 | async-start | bytes 8388608
  374.6 12.2 %copy-start.20 = (bf16[576,1024]{1,0:T(8,128)(2,1)S(1)}, bf16[576,1024]{1,0:T(8,128)(2,1)}, u32[]{:S(2)}) copy-start(bf16[576,1024]{1,0:T(8,128)(2,1)} %copy-done.19) | copy-start | bytes 3538948
  374.6 12.2 %copy-start.22 = (bf16[512,1024]{1,0:T(8,128)(2,1)S(1)}, bf16[512,1024]{1,0:T(8,128)(2,1)}, u32[]{:S(2)}) copy-start(bf16[512,1024]{1,0:T(8,128)(2,1)} %attend_cont.1) | copy-start | bytes 3145732
  374.6 12.2 %copy-start.34 = (bf16[64,1024]{1,0:T(8,128)(2,1)S(1)}, bf16[64,1024]{1,0:T(8,128)(2,1)}, u32[]{:S(2)}) copy-start(bf16[64,1024]{1,0:T(8,128)(2,1)} %attend_prompt.1) | copy-start | bytes 393220
  390.1 8.4 %slice-start.2 = ((s8[9437184]{0:T(1024)(128)(4,1)}), s8[4194304]{0:T(1024)(128)(4,1)S(1)}, s32[]{:S(2)}) async-start(s8[9437184]{0:T(1024)(128)(4,1)} %bitcast.285), calls=%async_computation.2 | async-start | bytes 8388608
  390.1 8.4 %slice-start.3 = ((s8[9437184]{0:T(1024)(128)(4,1)}), s8[4194304]{0:T(1024)(128)(4,1)S(1)}, s32[]{:S(2)}) async-start(s8[9437184]{0:T(1024)(128)(4,1)} %bitcast.285), calls=%async_computation.3 | async-start | bytes 8388608
  398.6 10.7 %copy-start.6 = (bf16[576,1024]{1,0:T(8,128)(2,1)S(1)}, bf16[576,1024]{1,0:T(8,128)(2,1)}, u32[]{:S(2)}) copy-start(bf16[576,1024]{1,0:T(8,128)(2,1)} %copy-done.5) | copy-start | bytes 3538948
  398.6 10.7 %copy-start.27 = (bf16[576,1024]{1,0:T(8,128)(2,1)S(1)}, bf16[576,1024]{1,0:T(8,128)(2,1)}, u32[]{:S(2)}) copy-start(bf16[576,1024]{1,0:T(8,128)(2,1)} %copy-done.26) | copy-start | bytes 3538948
  412.4 150.4 %copy-start.49 = (f32[64]{0:T(128)S(1)}, f32[64]{0:T(128)}, u32[]{:S(2)}) copy-start(f32[64]{0:T(128)} %copy-done.48) | copy-start | bytes 772
  571.0 14.5 %copy-start.38 = (f32[32,1024]{1,0:T(8,128)S(1)}, f32[32,1024]{1,0:T(8,128)}, u32[]{:S(2)}) copy-start(f32[32,1024]{1,0:T(8,128)} %get-tuple-element.169) | copy-start | bytes 393220
  571.0 15.2 %copy-start.37 = (f32[32,1024]{1,0:T(8,128)S(1)}, f32[32,1024]{1,0:T(8,128)}, u32[]{:S(2)}) copy-start(f32[32,1024]{1,0:T(8,128)} %get-tuple-element.170) | copy-start | bytes 393220
  571.0 15.8 %copy-start.36 = (f32[32,1024]{1,0:T(8,128)S(1)}, f32[32,1024]{1,0:T(8,128)}, u32[]{:S(2)}) copy-start(f32[32,1024]{1,0:T(8,128)} %get-tuple-element.171) | copy-start | bytes 393220
  571.0 16.5 %copy-start.35 = (f32[32,1024]{1,0:T(8,128)S(1)}, f32[32,1024]{1,0:T(8,128)}, u32[]{:S(2)}) copy-start(f32[32,1024]{1,0:T(8,128)} %get-tuple-element.172) | copy-start | bytes 393220
  581.7 6.4 %copy-start.29 = (f32[32,4096]{1,0:T(8,128)S(1)}, f32[32,4096]{1,0:T(8,128)}, u32[]{:S(2)}) copy-start(f32[32,4096]{1,0:T(8,128)} %get-tuple-element.173) | copy-start | bytes 1572868
  581.7 7.2 %copy-start.28 = (f32[128,1024]{1,0:T(8,128)S(1)}, f32[128,1024]{1,0:T(8,128)}, u32[]{:S(2)}) copy-start(f32[128,1024]{1,0:T(8,128)} %get-tuple-element.174) | copy-start | bytes 1572868
  (40 other events, 128.5 us)
